TPU v7x, 32 devices: a whole 2x2x4 slice. The times are simulated.
32 devices in a mesh: grp: 2 (over y), ka: 4 (over z), vib: 2 (over core), fin: 2 (over x).
Axes of the slice: x: 2, y: 2, z: 4, core: 2. Of those that a mesh axis runs over, the one named last changes fastest.
Arguments:
- moments: bfloat16 [2, 2048, 2048], P(None, 'vib'), may hold values from -0.125 to 0.125
- initial_vectors: bfloat16 [8, 2048, 2048], P('ka', 'vib', 'grp'), parts along dimension 2, may hold values from -6 to 6
- final_vectors: bfloat16 [8, 2048, 1024], P('ka', 'vib', ('grp', 'fin')), parts along dimension 2, may hold values from -0.046875 to 0.046875
- basis_counts: int32 [16], P(('grp', 'ka')), parts along dimension 0, may hold values from 512 to 2048
Outputs:
- strengths: float32 [2048, 512], P(('grp', 'ka', 'vib'), 'fin'), parts along dimension 0
There are 2 independent parts, one for each index of `grp`. A program takes and returns all parts, laid end to end along the dimension named above; an argument that names none is the same for every part. Nothing has to cross between parts.
All inputs are finite; a program needn't handle non-finite values.
Results may differ from a plain program's by a relative error of at most 0.0003.
Values may be sent and summed in bfloat16 or wider, within the bound.
No kernel may reach another device: no remote copies, remote signals or barrier semaphores. Data moves between devices by JAX's collectives and lax.ppermute only.
A program may use at most 64 MiB of HBM per device.

v0:
```python
import jax
import jax.numpy as jnp
from jax import lax
from jax.sharding import PartitionSpec as P

JQ = 30


def extended(shard, sides, width):
    for axis, dim in sides:
        size, length = (lax.axis_size(axis), shard.shape[dim])
        up = [(i, (i + 1) % size) for i in range(size - 1)]
        down = [(j, i) for i, j in up]
        last = lax.slice_in_dim(shard, length - width, length, axis=dim)
        initial = lax.slice_in_dim(shard, 0, width, axis=dim)
        before = lax.ppermute(last, axis, up)
        after = lax.ppermute(initial, axis, down)
        shard = jnp.concatenate([before, shard, after], axis=dim)
    return shard


def coefficients(first_block, count, total_blocks):
    jsquare = float(JQ * (JQ + 1))
    norm_j = jnp.sqrt(jnp.float32(jsquare))
    k_index = first_block + jnp.arange(count, dtype=jnp.int32) - total_blocks // 2
    k_value = k_index.astype(jnp.float32)
    coef_same = k_value / norm_j
    coef_upper = 0.5 * jnp.sqrt(jsquare - k_value * (k_value + 1.0)) / norm_j
    coef_lower = -0.5 * jnp.sqrt(jsquare - k_value * (k_value - 1.0)) / norm_j
    return (coef_same, coef_upper, coef_lower)


def on_device(moments, initial_vectors, final_vectors, basis_counts):
    kblocks, vib_rows, states = initial_vectors.shape
    total_blocks = kblocks * lax.axis_size("ka")
    first_block = lax.axis_index("ka") * kblocks
    row_index = lax.axis_index("vib") * vib_rows + jnp.arange(vib_rows, dtype=jnp.int32)
    keep_mask = row_index[None, :] < basis_counts[:, None]
    initial_live = jnp.where(
        keep_mask[:, :, None], initial_vectors, jnp.zeros((), initial_vectors.dtype)
    )
    final_live = jnp.where(keep_mask[:, :, None], final_vectors, jnp.zeros((), final_vectors.dtype))
    final_whole = lax.all_gather(final_live, "vib", axis=1, tiled=True)
    images = jnp.einsum("cvw,kwf->vkcf", moments, final_whole, preferred_element_type=jnp.float32)
    widened = extended(images[:, :, 1], (("ka", 1),), 1)
    ext_same, ext_upper, ext_lower = coefficients(first_block - 1, kblocks + 2, total_blocks)
    coef_same = ext_same[1:-1]
    combined = (
        coef_same[None, :, None] * images[:, :, 0]
        + ext_upper[:-2][None, :, None] * widened[:, :-2]
        + ext_lower[2:][None, :, None] * widened[:, 2:]
    )
    amplitude = jnp.einsum(
        "kvi,vkf->if", initial_live.astype(jnp.float32), combined, precision=lax.Precision.HIGHEST
    )
    summed = lax.psum(amplitude, ("ka", "vib"))
    row_share = states // lax.axis_size(("ka", "vib"))
    amplitude = lax.dynamic_slice_in_dim(
        summed, lax.axis_index(("ka", "vib")) * row_share, row_share, 0
    )
    return amplitude * amplitude


def solution(mesh):
    in_specs = (
        P(None, "vib", None),
        P("ka", "vib", "grp"),
        P("ka", "vib", ("grp", "fin")),
        P(("grp", "ka")),
    )
    out_specs = P(("grp", "ka", "vib"), "fin")
    return jax.shard_map(
        on_device, mesh=mesh, in_specs=in_specs, out_specs=out_specs, check_vma=False
    )
```

profile of v0, /device:TPU:0, one launch (start us, length us, event | category | flops | bytes accessed | tf_op | source)
XLA Modules:
  0.0 141.9 jit_solution(8668482068040856457)
XLA Ops:
  6.5 0.0 copy-start.1
  6.5 0.0 all-gather.2.cloned.1.call-start
  6.5 1.5 %copy.5 = bf16[2,1024,256]{1,2,0:T(8,128)(2,1)S(1)} copy(bf16[2,1024,256]{2,1,0:T(8,128)(2,1)} %param.6) | data formatting | bytes 2097152 | tf_op args[2]
  8.0 0.0 copy-done.1
  8.0 0.1 broadcast_compare_fusion
  8.1 1.1 broadcast_select_fusion
  9.2 0.0 all-gather.2.cloned.1.call-update
  9.2 0.0 all-reduce.2.cloned.1.call-start
  9.3 13.4 %all-gather.2.cloned.1.call-done = bf16[2,2048,256]{1,2,0:T(8,128)(2,1)} async-done(((bf16[2,1024,256]{1,2,0:T(8,128)(2,1)}), bf16[2,2048,256]{1,2,0:T(8,128)(2,1)}) %all-gather.2.cloned.1.call-update) | async-done | bytes 2097168 | tf_op jit(solution)/shard_map/all_gather | solution.py:43
  22.7 7.6 %fusion.5 = f32[1024,2,2,256]{0,3,2,1:T(8,128)S(1)} fusion(bf16[2,1024,2048]{2,1,0:T(8,128)(2,1)} %param.4, bf16[2,2048,256]{1,2,0:T(8,128)(2,1)} %all-gather.2.cloned.1.call-done), kind=kOutput, calls=%fused_computation.5 | convolution fusion | flops 4294967296 | bytes 14680064 | tf_op jit(solution)/shard_map/cvw,kwf->vkcf/dot_general | solution.py:44
  30.3 0.0 copy-start
  30.3 0.1 slice_bitcast_fusion
  30.5 1.8 %copy-done = f32[1024,2,2,256]{0,3,2,1:T(8,128)} copy-done((f32[1024,2,2,256]{0,3,2,1:T(8,128)}, f32[1024,2,2,256]{0,3,2,1:T(8,128)S(1)}, u32[]{:S(2)}) %copy-start) | copy-done | bytes 4194328
  32.3 1.2 fusion.36
  33.4 4.7 %collective-permute-start = (f32[1024,1,256]{0,2,1:T(8,128)}, f32[1024,1,256]{0,2,1:T(8,128)}, u32[]{:S(2)}, u32[]{:S(2)}) collective-permute-start(f32[1024,1,256]{0,2,1:T(8,128)} %get-tuple-element.5), channel_id=1, source_target_pairs={{0,4},{4,8},{8,12},{1,5},{5,9},{9,13},{2,6},{6,10},{10,14},{3,7},{... | collective-permute-start | bytes 3145736 | tf_op jit(solution)/shard_map/ppermute | solution.py:16
  38.1 1.3 collective-permute-start.1
  39.4 0.1 slice.35
  39.5 0.1 slice.29
  39.6 20.7 %collective-permute-done = f32[1024,1,256]{0,2,1:T(8,128)} collective-permute-done((f32[1024,1,256]{0,2,1:T(8,128)}, f32[1024,1,256]{0,2,1:T(8,128)}, u32[]{:S(2)}, u32[]{:S(2)}) %collective-permute-start) | collective-permute-done | bytes 1048608 | tf_op jit(solution)/shard_map/ppermute | solution.py:16
  60.3 4.9 %collective-permute-done.1 = f32[1024,1,256]{0,2,1:T(8,128)} collective-permute-done((f32[1024,1,256]{0,2,1:T(8,128)S(1)}, f32[1024,1,256]{0,2,1:T(8,128)}, u32[]{:S(2)}, u32[]{:S(2)}) %collective-permute-start.1) | collective-permute-done | bytes 1048608 | tf_op jit(solution)/shard_map/ppermute | solution.py:17
  65.2 9.9 %fusion.20 = f32[1024,256]{1,0:T(8,128)} fusion(f32[1024,1,256]{0,2,1:T(8,128)} %collective-permute-done.1, f32[1024,2,256]{0,2,1:T(8,128)S(1)} %slice_bitcast_fusion, f32[1024,1,256]{0,2,1:T(8,128)} %collective-permute-done, f32[1024,2,2,256]{0,3,2,1:T(8,128)} %copy-done, bf16[2,1024,1024]{2,1,0:T(8,128)(2,1)} %param.5, ...), kind=kOutput, calls=%fused_computation.19 | convolution fusion | flops 6448218112 | bytes 11536408 | tf_op jit(solution)/shard_map/kvi,vkf->if/dot_general | solution.py:53
  75.0 0.0 all-reduce.2.cloned.1.call-update
  75.1 58.5 %all-reduce.2.cloned.1.call-done = f32[1024,256]{1,0:T(8,128)} async-done(((f32[1024,256]{1,0:T(8,128)}), f32[1024,256]{1,0:T(8,128)}) %all-reduce.2.cloned.1.call-update) | async-done | bytes 1048592 | tf_op jit(solution)/shard_map/psum | solution.py:56
  133.5 1.6 %dynamic-slice_multiply_fusion = f32[128,256]{1,0:T(8,128)} fusion(f32[1024,256]{1,0:T(8,128)} %all-reduce.2.cloned.1.call-done, s32[]{:T(128)S(6)} %select_n.13), kind=kLoop, calls=%fused_computation.24 | loop fusion | flops 32768 | bytes 262148 | tf_op jit(solution)/shard_map/mul | solution.py:61
  (3 shorter events, 0.0 us)
Async XLA Ops:
  6.5 1.5 %copy-start.1 = (s32[2]{0:T(128)S(1)}, s32[2]{0:T(128)}, u32[]{:S(2)}) copy-start(s32[2]{0:T(128)} %param.7) | copy-start | bytes 28
  6.5 16.1 %all-gather.2.cloned.1.call-start = ((), (), s32[]{:S(2)}) async-start(), calls=%async_computation | async-start | bytes 3145728 | tf_op jit(solution)/shard_map/all_gather | solution.py:43
  9.2 124.3 %all-reduce.2.cloned.1.call-start = ((), (), s32[]{:S(2)}) async-start(), calls=%async_computation.1 | async-start | bytes 2097152 | tf_op jit(solution)/shard_map/psum | solution.py:56
  30.3 1.9 %copy-start = (f32[1024,2,2,256]{0,3,2,1:T(8,128)}, f32[1024,2,2,256]{0,3,2,1:T(8,128)S(1)}, u32[]{:S(2)}) copy-start(f32[1024,2,2,256]{0,3,2,1:T(8,128)S(1)} %fusion.5) | copy-start | bytes 12582916
  33.4 26.8 %collective-permute-start = (f32[1024,1,256]{0,2,1:T(8,128)}, f32[1024,1,256]{0,2,1:T(8,128)}, u32[]{:S(2)}, u32[]{:S(2)}) collective-permute-start(f32[1024,1,256]{0,2,1:T(8,128)} %get-tuple-element.5), channel_id=1, source_target_pairs={{0,4},{4,8},{8,12},{1,5},{5,9},{9,13},{2,6},{6,10},{10,14},{3,7},{... | collective-permute-start | bytes 3145736 | tf_op jit(solution)/shard_map/ppermute | solution.py:16
  38.1 27.1 %collective-permute-start.1 = (f32[1024,1,256]{0,2,1:T(8,128)S(1)}, f32[1024,1,256]{0,2,1:T(8,128)}, u32[]{:S(2)}, u32[]{:S(2)}) collective-permute-start(f32[1024,1,256]{0,2,1:T(8,128)S(1)} %get-tuple-element.6), channel_id=1, source_target_pairs={{4,0},{8,4},{12,8},{5,1},{9,5},{13,9},{6,2},{10,6},{14,10},{7,3},{... | collective-permute-start | bytes 3145736 | tf_op jit(solution)/shard_map/ppermute | solution.py:17
Sparse Core Ops, SparseCore 0:
  9.3 13.2 all-gather.1
  75.2 58.2 all-reduce.1
where the time goes:
time: 142 us
  waiting for transfers between devices  97.5 us (69%)
  matrix products  17.5 us (12%)
  between operations  13.5 us (10%)
  starting transfers between devices  5.98 us (4%)
  local copies, waits for them, and re-layouts  4.75 us (3%)
  other arithmetic  2.73 us (2%)
    psum x1, waiting for transfers between devices, on_device(): summed = lax.psum(amplitude, ('ka', 'vib'))  58.5 us
    ppermute x1, waiting for transfers between devices, extended(): before = lax.ppermute(last, axis, up)  20.7 us
    all_gather x1, waiting for transfers between devices, on_device(): final_whole = lax.all_gather(final_live, 'vib', axis=1, tiled=True)  13.4 us
    dot_general x1, matrix products, on_device(): jnp.einsum('kvi,vkf->if', initial_live.astype(jnp.float32), combined, pre...  9.88 us
    dot_general x1, matrix products, on_device(): jnp.einsum('cvw,kwf->vkcf', moments, final_whole, preferred_element_type=...  7.63 us
    ppermute x1, waiting for transfers between devices, extended(): after = lax.ppermute(initial, axis, down)  4.89 us
    ppermute x1, starting transfers between devices, extended(): before = lax.ppermute(last, axis, up)  4.65 us
    unnamed x5, local copies, waits for them, and re-layouts  3.29 us
  transfers between devices with their start and end apart: 4, of which 4 were waited for; matrix products, arithmetic and copies ran while one was open for 0% of the time, Pallas kernels for 0%

commit v1 on v0

v1 whole, which is shorter than its diff:
```python
import functools

import jax
import jax.numpy as jnp
import numpy as np
from jax import lax
from jax.experimental import pallas as pl
from jax.experimental.pallas import tpu as pltpu
from jax.sharding import PartitionSpec as P

JQ = 30
CHUNKS = 1
BF16, F32 = jnp.bfloat16, jnp.float32


def coefficient_table(positions, kblocks):
    total = positions * kblocks
    jsquare = np.float32(JQ * (JQ + 1))
    norm = np.sqrt(jsquare)
    k = (np.arange(total) - total // 2).astype(np.float32)
    same = k / norm
    upper = np.float32(0.5) * np.sqrt(jsquare - k * (k + np.float32(1.0))) / norm
    lower = np.float32(-0.5) * np.sqrt(jsquare - k * (k - np.float32(1.0))) / norm
    rows = []
    for a in range(positions):
        first, last = a * kblocks, a * kblocks + 1
        before = upper[first - 1] if first > 0 else 0.0
        after = lower[last + 1] if last + 1 < total else 0.0
        rows.append([same[first], same[last], lower[last], upper[first], before, after, 0.0, 0.0])
    return np.asarray(rows, np.float32)


def mask_rows(x, count, start):
    row = lax.broadcasted_iota(jnp.int32, x.shape, 0) + start
    return jnp.where(row < count, x.astype(F32), 0.0).astype(x.dtype)


def pack_kernel(chunks, place, counts, final, *outs):
    parity, core = place[0], place[1]
    rows, width = final.shape[1], final.shape[2] // chunks
    for slot in range(2):
        k = 1 - parity if slot == 0 else parity
        block = mask_rows(final[k], counts[k], core * rows)
        for c in range(chunks):
            outs[2 * c + slot][...] = block[:, c * width : (c + 1) * width]


def own_kernel(chunks, place, counts, coefs, moments, mine, other, *rest):
    outs, rhs = rest[:chunks], rest[chunks]
    core = place[1]
    kblocks, rows, states = mine.shape
    width = states // chunks

    @pl.when(pl.program_id(0) == 0)
    def _():
        for half, source in ((core, mine), (1 - core, other)):
            start = pl.multiple_of(half * rows, rows)
            for k in range(kblocks):
                block = mask_rows(source[k], counts[k], start)
                for c in range(chunks):
                    at = (c * kblocks + k) * width
                    rhs[pl.ds(start, rows), at : at + width] = block[:, c * width : (c + 1) * width]

    z = jnp.dot(moments[0], rhs[...], preferred_element_type=F32)
    x = jnp.dot(moments[1], rhs[...], preferred_element_type=F32)
    for c in range(chunks):
        lo, mid, hi = (2 * c) * width, (2 * c + 1) * width, (2 * c + 2) * width
        outs[c][:, :width] = coefs[0] * z[:, lo:mid] + coefs[2] * x[:, mid:hi]
        outs[c][:, width:] = coefs[1] * z[:, mid:hi] + coefs[3] * x[:, lo:mid]


def transpose_kernel(x, out):
    out[...] = x[0].T


def halo_kernel(
    places, place, counts, coefs, moments, pair_mine, pair_other, next_mine, next_other,
    partial, init_low, init_high, to_other, to_own, rhs, total,
):
    parity, core, position = place[0], place[1], place[2]
    rows, width = pair_mine.shape
    step, steps = pl.program_id(0), pl.num_programs(0)

    @pl.when(step == 0)
    def _():
        pair_at = pl.multiple_of((1 - parity) * width, width)
        next_at = pl.multiple_of(parity * width, width)
        mine_at = pl.multiple_of(core * rows, rows)
        other_at = pl.multiple_of((1 - core) * rows, rows)
        rhs[pl.ds(mine_at, rows), pl.ds(pair_at, width)] = pair_mine[...]
        rhs[pl.ds(other_at, rows), pl.ds(pair_at, width)] = pair_other[...]
        rhs[pl.ds(mine_at, rows), pl.ds(next_at, width)] = next_mine[...]
        rhs[pl.ds(other_at, rows), pl.ds(next_at, width)] = next_other[...]
        total[...] = jnp.zeros_like(total)

    x = jnp.dot(moments[0], rhs[...], preferred_element_type=F32)
    block = x.shape[0]
    row = lax.broadcasted_iota(jnp.int32, (block, width), 0) + core * rows + step * block
    for k, init in ((0, init_low), (1, init_high)):
        cols = slice(k * width, (k + 1) * width)
        image = partial[:, cols] + coefs[4 + k] * x[:, cols]
        image = jnp.where(row < counts[k], image, 0.0)
        high = image.astype(BF16)
        low = (image - high.astype(F32)).astype(BF16)
        both = jnp.dot(init[...], jnp.concatenate([high, low], axis=1), preferred_element_type=F32)
        total[...] += both[:, :width] + both[:, width:]

    @pl.when(step == steps - 1)
    def _():
        share = to_own.shape[0] // places
        for s in range(places):
            dest = lax.rem(position + s, places)
            own_at = pl.multiple_of((dest * 2 + core) * share, share)
            other_at = pl.multiple_of((dest * 2 + 1 - core) * share, share)
            to_own[s * share : (s + 1) * share, :] = total[pl.ds(own_at, share), :]
            to_other[s * share : (s + 1) * share, :] = total[pl.ds(other_at, share), :]


def add_kernel(mine, other, *outs):
    share = outs[0].shape[0]
    for s, out in enumerate(outs):
        rows = slice(s * share, (s + 1) * share)
        out[...] = mine[rows, :] + other[rows, :]


def finish_kernel(places, *refs):
    out = refs[-1]
    width = refs[0].shape[1]
    for c in range((len(refs) - 1) // places):
        terms = refs[c * places : (c + 1) * places]
        amplitude = terms[0][...]
        for term in terms[1:]:
            amplitude = amplitude + term[...]
        out[:, c * width : (c + 1) * width] = amplitude * amplitude


def cost(flops, moved):
    return pl.CostEstimate(flops=int(flops), bytes_accessed=int(moved), transcendentals=0)


def on_device(moments, initial_vectors, final_vectors, basis_counts):
    kblocks, rows, states = initial_vectors.shape
    finals = final_vectors.shape[2]
    whole = moments.shape[2]
    places, cores = lax.axis_size("ka"), lax.axis_size("vib")
    if kblocks != 2 or cores != 2 or places % 2:
        raise ValueError("unsupported mesh")
    chunks = CHUNKS if finals % (CHUNKS * 128) == 0 else 1
    width = finals // chunks
    share = states // (places * cores)

    position, core = lax.axis_index("ka"), lax.axis_index("vib")
    table = np.asarray(
        [[a % 2, b, a, 0] for a in range(places) for b in range(cores)], np.int32
    )
    place = lax.dynamic_index_in_dim(jnp.asarray(table), position * cores + core, 0, False)
    coefs = lax.dynamic_index_in_dim(
        jnp.asarray(coefficient_table(places, kblocks)), position, 0, False
    )

    swap = [(0, 1), (1, 0)]
    pair = [(a, a + 1 - 2 * (a % 2)) for a in range(places)]
    other_side = [(a, min(max(a - 1 + 2 * (a % 2), 0), places - 1)) for a in range(places)]
    smem = pl.BlockSpec(memory_space=pltpu.SMEM)
    vmem = pl.BlockSpec(memory_space=pltpu.VMEM)

    final_other = lax.ppermute(final_vectors, "vib", swap)

    payload = pl.pallas_call(
        functools.partial(pack_kernel, chunks),
        out_shape=[jax.ShapeDtypeStruct((rows, width), BF16)] * (2 * chunks),
        in_specs=[smem, smem, vmem],
        out_specs=[vmem] * (2 * chunks),
        cost_estimate=cost(0, 4 * kblocks * rows * finals),
        name="pack",
    )(place, basis_counts, final_vectors)
    halo = []
    for c in range(chunks):
        near = lax.ppermute(payload[2 * c], "ka", pair)
        far = lax.ppermute(payload[2 * c + 1], "ka", other_side)
        halo.append((near, far))

    tile = 256
    init_t = pl.pallas_call(
        transpose_kernel,
        out_shape=jax.ShapeDtypeStruct((states, kblocks * rows), BF16),
        grid=(kblocks, rows // tile),
        in_specs=[pl.BlockSpec((1, tile, states), lambda k, j: (k, j, 0))],
        out_specs=pl.BlockSpec((states, tile), lambda k, j: (0, k * (rows // tile) + j)),
        cost_estimate=cost(0, 4 * kblocks * rows * states),
        name="turn",
    )(initial_vectors)

    block = 256
    partial = pl.pallas_call(
        functools.partial(own_kernel, chunks),
        out_shape=[jax.ShapeDtypeStruct((rows, kblocks * width), F32)] * chunks,
        grid=(rows // block,),
        in_specs=[
            smem,
            smem,
            smem,
            pl.BlockSpec((2, block, whole), lambda j: (0, j, 0)),
            pl.BlockSpec((kblocks, rows, finals), lambda j: (0, 0, 0)),
            pl.BlockSpec((kblocks, rows, finals), lambda j: (0, 0, 0)),
        ],
        out_specs=[pl.BlockSpec((block, kblocks * width), lambda j: (j, 0))] * chunks,
        scratch_shapes=[pltpu.VMEM((whole, kblocks * finals), BF16)],
        cost_estimate=cost(
            4 * rows * whole * kblocks * finals, 2 * moments.size + 8 * rows * finals
        ),
        name="own",
    )(place, basis_counts, coefs, moments, final_vectors, final_other)

    blocks = []
    for c in range(chunks):
        near, far = halo[c]
        near_other = lax.ppermute(near, "vib", swap)
        far_other = lax.ppermute(far, "vib", swap)
        half = states // cores
        to_other, to_own = pl.pallas_call(
            functools.partial(halo_kernel, places),
            out_shape=[jax.ShapeDtypeStruct((half, width), F32)] * 2,
            grid=(rows // block,),
            in_specs=[
                smem,
                smem,
                smem,
                pl.BlockSpec((1, block, whole), lambda j: (1, j, 0)),
                *[pl.BlockSpec((rows, width), lambda j: (0, 0))] * 4,
                pl.BlockSpec((block, kblocks * width), lambda j: (j, 0)),
                pl.BlockSpec((states, block), lambda j: (0, j)),
                pl.BlockSpec((states, block), lambda j: (0, rows // block + j)),
            ],
            out_specs=[pl.BlockSpec((half, width), lambda j: (0, 0))] * 2,
            scratch_shapes=[
                pltpu.VMEM((whole, kblocks * width), BF16),
                pltpu.VMEM((states, width), F32),
            ],
            cost_estimate=cost(
                2 * rows * whole * kblocks * width + 8 * rows * states * width,
                moments.size + 4 * rows * states,
            ),
            name="halo",
        )(
            place, basis_counts, coefs, moments, near, near_other, far, far_other,
            partial[c], init_t, init_t,
        )
        received = lax.ppermute(to_other, "vib", swap)
        sums = pl.pallas_call(
            add_kernel,
            out_shape=[jax.ShapeDtypeStruct((share, width), F32)] * places,
            in_specs=[vmem] * 2,
            out_specs=[vmem] * places,
            cost_estimate=cost(0, 12 * half * width),
            name="add",
        )(to_own, received)
        blocks.append(sums[0])
        for s in range(1, places):
            turn = [(a, (a + s) % places) for a in range(places)]
            blocks.append(lax.ppermute(sums[s], "ka", turn))

    return pl.pallas_call(
        functools.partial(finish_kernel, places),
        out_shape=jax.ShapeDtypeStruct((share, finals), F32),
        in_specs=[vmem] * len(blocks),
        out_specs=vmem,
        cost_estimate=cost(0, 4 * share * finals * (places + 1)),
        name="finish",
    )(*blocks)


def solution(mesh):
    in_specs = (
        P(None, "vib", None),
        P("ka", "vib", "grp"),
        P("ka", "vib", ("grp", "fin")),
        P(("grp", "ka")),
    )
    out_specs = P(("grp", "ka", "vib"), "fin")
    return jax.shard_map(
        on_device, mesh=mesh, in_specs=in_specs, out_specs=out_specs, check_vma=False
    )
```

time: 142 us -> 74 us (0.52)
  the two profiles are of different devices: /device:TPU:0 before, /device:TPU:24 now
where the time goes in v1:
time: 74 us; the launch traced here: 73.5 us
  Pallas kernels  32.6 us (44%)
  waiting for transfers between devices  26.4 us (36%)
  starting transfers between devices  7.92 us (11%)
  local copies, waits for them, and re-layouts  6.54 us (9%)
    ppermute x1, waiting for transfers between devices, on_device(): near = lax.ppermute(payload[2 * c], 'ka', pair)  12.4 us
    ppermute x3, waiting for transfers between devices, on_device(): blocks.append(lax.ppermute(sums[s], 'ka', turn))  12 us
    pallas_call x1, Pallas kernels, on_device(): pl.pallas_call(functools.partial(halo_kernel, places), out_shape=[jax.Sha...  9.93 us
    pallas_call x1, Pallas kernels, on_device(): pl.pallas_call(functools.partial(own_kernel, chunks), out_shape=[jax.Shap...  9.25 us
    pallas_call x1, Pallas kernels, on_device(): pl.pallas_call(transpose_kernel, out_shape=jax.ShapeDtypeStruct((states,...  7.31 us
    ppermute x3, starting transfers between devices, on_device(): blocks.append(lax.ppermute(sums[s], 'ka', turn))  5.07 us
    unnamed x18, local copies, waits for them, and re-layouts  4.13 us
    pallas_call x1, Pallas kernels, on_device(): pl.pallas_call(functools.partial(pack_kernel, chunks), out_shape=[jax.Sha...  2.35 us
  transfers between devices with their start and end apart: 9, of which 4 were waited for; matrix products, arithmetic and copies ran while one was open for 3% of the time, Pallas kernels for 26%

profile of v1, /device:TPU:24, one launch (start us, length us, event | category | flops | bytes accessed | tf_op | source)
XLA Modules:
  0.0 73.5 jit_solution(4375134573237289992)
XLA Ops:
  0.0 0.0 collective-permute-start.4
  0.0 1.2 %dynamic-slice_bitcast_fusion.1.place = s32[4]{0:T(128)} fusion(s32[8,4]{1,0:T(8,128)} %constant.26.clone, s32[]{:T(128)S(6)} %select_n.8), kind=kLoop, calls=%fused_computation.1 | loop fusion | bytes 36 | tf_op jit(solution)/shard_map/jit(dynamic_index_in_dim)/squeeze | solution.py:156
  1.2 2.3 %pack.1 = (bf16[1024,256]{1,0:T(8,128)(2,1)}, bf16[1024,256]{1,0:T(8,128)(2,1)}) custom-call(s32[4]{0:T(128)} %dynamic-slice_bitcast_fusion.1.place, s32[2]{0:T(128)} %counts.5, bf16[2,1024,256]{2,1,0:T(8,128)(2,1)} %mine.1), custom_call_target="tpu_custom_call" | custom-call | bytes 2097152 | tf_op jit(solution)/shard_map/pack/pallas_call | solution.py:169
  3.6 0.4 collective-permute-start
  4.0 1.7 %collective-permute-start.2 = (bf16[1024,256]{1,0:T(8,128)(2,1)}, bf16[1024,256]{1,0:T(8,128)(2,1)S(1)}, u32[]{:S(2)}, u32[]{:S(2)}) collective-permute-start(bf16[1024,256]{1,0:T(8,128)(2,1)} %get-tuple-element.14), channel_id=1, source_target_pairs={{0,0},{4,8},{8,4},{12,12},{1,1},{5,9},{9,5},{13,13},{2,2},{6,10},{... | collective-permute-start | bytes 1572872 | tf_op jit(solution)/shard_map/ppermute | solution.py:180
  5.7 12.4 %collective-permute-done.pair_mine = bf16[1024,256]{1,0:T(8,128)(2,1)S(1)} collective-permute-done((bf16[1024,256]{1,0:T(8,128)(2,1)}, bf16[1024,256]{1,0:T(8,128)(2,1)S(1)}, u32[]{:S(2)}, u32[]{:S(2)}) %collective-permute-start) | collective-permute-done | bytes 524320 | tf_op jit(solution)/shard_map/ppermute | solution.py:179
  18.1 0.0 copy-start
  18.1 0.0 collective-permute-start.1
  18.1 0.0 collective-permute-done.2.next_mine
  18.1 0.0 copy-start.1
  18.1 0.5 collective-permute-start.3
  18.6 7.3 %turn.1.init_low.init_high = bf16[1024,2048]{1,0:T(8,128)(2,1)} custom-call(bf16[2,1024,1024]{2,1,0:T(8,128)(2,1)} %x.1), custom_call_target="tpu_custom_call" | custom-call | bytes 8388608 | tf_op jit(solution)/shard_map/turn/pallas_call | solution.py:184
  25.9 0.0 copy-done
  25.9 0.0 copy-done.1
  25.9 1.2 %dynamic-slice_bitcast_fusion.coefs = f32[8]{0:T(128)} fusion(f32[4,8]{1,0:T(4,128)} %constant.27.clone, s32[]{:T(128)S(6)} %select_n.9), kind=kLoop, calls=%fused_computation | loop fusion | bytes 68 | tf_op jit(solution)/shard_map/jit(dynamic_index_in_dim)/squeeze | solution.py:157
  27.1 0.0 collective-permute-done.4.other
  27.1 0.0 copy-start.8
  27.1 1.0 %copy-done.8 = bf16[2,1024,256]{2,1,0:T(8,128)(2,1)} copy-done((bf16[2,1024,256]{2,1,0:T(8,128)(2,1)}, bf16[2,1024,256]{2,1,0:T(8,128)(2,1)S(1)}, u32[]{:S(2)}) %copy-start.8) | copy-done | bytes 1048600
  28.1 9.2 %own.1.partial = f32[1024,512]{1,0:T(8,128)} custom-call(s32[4]{0:T(128)} %dynamic-slice_bitcast_fusion.1.place, s32[2]{0:T(128)} %counts.5, f32[8]{0:T(128)} %dynamic-slice_bitcast_fusion.coefs, bf16[2,1024,2048]{2,1,0:T(8,128)(2,1)} %moments.3, bf16[2,1024,256]{2,1,0:T(8,128)(2,1)} %mine.1, bf16[2,1024,256]{2,1,0:T(8,128)(2,1)} %copy-done.8), custom_call_target="tpu_custom_call" | custom-call | flops 4294967296 | bytes 10485760 | tf_op jit(solution)/shard_map/own/pallas_call | solution.py:195
  37.4 0.0 collective-permute-done.1.pair_other
  37.4 0.0 copy-start.2
  37.4 0.0 collective-permute-done.3.next_other
  37.4 0.8 %copy-done.2 = bf16[1024,256]{1,0:T(8,128)(2,1)} copy-done((bf16[1024,256]{1,0:T(8,128)(2,1)}, bf16[1024,256]{1,0:T(8,128)(2,1)S(1)}, u32[]{:S(2)}) %copy-start.2) | copy-done | bytes 524312
  38.2 0.0 copy-start.3
  38.2 0.9 %copy-done.3 = bf16[1024,256]{1,0:T(8,128)(2,1)} copy-done((bf16[1024,256]{1,0:T(8,128)(2,1)}, bf16[1024,256]{1,0:T(8,128)(2,1)S(1)}, u32[]{:S(2)}) %copy-start.3) | copy-done | bytes 524312
  39.0 9.9 %halo.1 = (f32[512,256]{1,0:T(8,128)}, f32[512,256]{1,0:T(8,128)}) custom-call(s32[4]{0:T(128)} %dynamic-slice_bitcast_fusion.1.place, s32[2]{0:T(128)} %counts.5, f32[8]{0:T(128)} %dynamic-slice_bitcast_fusion.coefs, bf16[2,1024,2048]{2,1,0:T(8,128)(2,1)} %moments.3, bf16[1024,256]{1,0:T(8,128)(2,1)} %copy-done, bf16[1024,256]{1,0:T(8,128)(2,1)} %copy-done.2, ...), custom_call_target="tpu_custom_call" | custom-call | flops 4294967296 | bytes 8388608 | tf_op jit(solution)/shard_map/halo/pallas_call | solution.py:221
  49.0 0.2 collective-permute-start.5
  49.2 1.9 %collective-permute-done.5.other = f32[512,256]{1,0:T(8,128)S(1)} collective-permute-done((f32[512,256]{1,0:T(8,128)}, f32[512,256]{1,0:T(8,128)S(1)}, u32[]{:S(2)}, u32[]{:S(2)}) %collective-permute-start.5) | collective-permute-done | bytes 524320 | tf_op jit(solution)/shard_map/ppermute | solution.py:249
  51.1 0.0 copy-start.4
  51.1 0.8 %copy-done.4 = f32[512,256]{1,0:T(8,128)} copy-done((f32[512,256]{1,0:T(8,128)}, f32[512,256]{1,0:T(8,128)S(1)}, u32[]{:S(2)}) %copy-start.4) | copy-done | bytes 524312
  51.9 2.0 %add.15 = (f32[128,256]{1,0:T(8,128)}, f32[128,256]{1,0:T(8,128)}, f32[128,256]{1,0:T(8,128)}, f32[128,256]{1,0:T(8,128)}) custom-call(f32[512,256]{1,0:T(8,128)} %get-tuple-element.15.mine, f32[512,256]{1,0:T(8,128)} %copy-done.4), custom_call_target="tpu_custom_call" | custom-call | bytes 1572864 | tf_op jit(solution)/shard_map/add/pallas_call | solution.py:250
  53.9 0.1 collective-permute-start.6
  53.9 4.7 %collective-permute-start.7 = (f32[128,256]{1,0:T(8,128)}, f32[128,256]{1,0:T(8,128)S(1)}, u32[]{:S(2)}, u32[]{:S(2)}) collective-permute-start(f32[128,256]{1,0:T(8,128)} %get-tuple-element.19), channel_id=1, source_target_pairs={{0,8},{4,12},{8,0},{12,4},{1,9},{5,13},{9,1},{13,5},{2,10},{6,14},... | collective-permute-start | bytes 393224 | tf_op jit(solution)/shard_map/ppermute | solution.py:261
  58.7 0.3 collective-permute-start.8
  58.9 2.4 %collective-permute-done.6.refs_1_ = f32[128,256]{1,0:T(8,128)S(1)} collective-permute-done((f32[128,256]{1,0:T(8,128)}, f32[128,256]{1,0:T(8,128)S(1)}, u32[]{:S(2)}, u32[]{:S(2)}) %collective-permute-start.6) | collective-permute-done | bytes 131104 | tf_op jit(solution)/shard_map/ppermute | solution.py:261
  61.4 0.0 copy-start.5
  61.4 9.6 %collective-permute-done.7.refs_2_ = f32[128,256]{1,0:T(8,128)S(1)} collective-permute-done((f32[128,256]{1,0:T(8,128)}, f32[128,256]{1,0:T(8,128)S(1)}, u32[]{:S(2)}, u32[]{:S(2)}) %collective-permute-start.7) | collective-permute-done | bytes 131104 | tf_op jit(solution)/shard_map/ppermute | solution.py:261
  71.0 0.0 copy-start.6
  71.0 0.0 collective-permute-done.8.refs_3_
  71.0 0.0 copy-start.7
  71.0 0.0 copy-done.5
  71.0 0.7 copy-done.6
  71.6 0.0 copy-done.7
  71.7 1.8 %finish.1 = f32[128,256]{1,0:T(8,128)} custom-call(f32[128,256]{1,0:T(8,128)} %get-tuple-element.17.refs_0_, f32[128,256]{1,0:T(8,128)} %copy-done.5, f32[128,256]{1,0:T(8,128)} %copy-done.6, f32[128,256]{1,0:T(8,128)} %copy-done.7), custom_call_target="tpu_custom_call" | custom-call | bytes 655360 | tf_op jit(solution)/shard_map/finish/pallas_call | solution.py:263
Async XLA Ops:
  0.0 27.1 %collective-permute-start.4 = (bf16[2,1024,256]{2,1,0:T(8,128)(2,1)}, bf16[2,1024,256]{2,1,0:T(8,128)(2,1)S(1)}, u32[]{:S(2)}, u32[]{:S(2)}) collective-permute-start(bf16[2,1024,256]{2,1,0:T(8,128)(2,1)} %mine.1), channel_id=1, source_target_pairs={{0,2},{2,0},{1,3},{3,1},{4,6},{6,4},{5,7},{7,5},{8,10},{10,8},{9,1... | collective-permute-start | bytes 3145736 | tf_op jit(solution)/shard_map/ppermute | solution.py:167
  3.6 14.5 %collective-permute-start = (bf16[1024,256]{1,0:T(8,128)(2,1)}, bf16[1024,256]{1,0:T(8,128)(2,1)S(1)}, u32[]{:S(2)}, u32[]{:S(2)}) collective-permute-start(bf16[1024,256]{1,0:T(8,128)(2,1)} %get-tuple-element.13), channel_id=1, source_target_pairs={{0,4},{4,0},{8,12},{12,8},{1,5},{5,1},{9,13},{13,9},{2,6},{6,2},{1... | collective-permute-start | bytes 1572872 | tf_op jit(solution)/shard_map/ppermute | solution.py:179
  4.0 14.1 %collective-permute-start.2 = (bf16[1024,256]{1,0:T(8,128)(2,1)}, bf16[1024,256]{1,0:T(8,128)(2,1)S(1)}, u32[]{:S(2)}, u32[]{:S(2)}) collective-permute-start(bf16[1024,256]{1,0:T(8,128)(2,1)} %get-tuple-element.14), channel_id=1, source_target_pairs={{0,0},{4,8},{8,4},{12,12},{1,1},{5,9},{9,5},{13,13},{2,2},{6,10},{... | collective-permute-start | bytes 1572872 | tf_op jit(solution)/shard_map/ppermute | solution.py:180
  18.1 7.8 %copy-start = (bf16[1024,256]{1,0:T(8,128)(2,1)}, bf16[1024,256]{1,0:T(8,128)(2,1)S(1)}, u32[]{:S(2)}) copy-start(bf16[1024,256]{1,0:T(8,128)(2,1)S(1)} %collective-permute-done.pair_mine) | copy-start | bytes 1572868
  18.1 19.3 %collective-permute-start.1 = (bf16[1024,256]{1,0:T(8,128)(2,1)S(1)}, bf16[1024,256]{1,0:T(8,128)(2,1)S(1)}, u32[]{:S(2)}, u32[]{:S(2)}) collective-permute-start(bf16[1024,256]{1,0:T(8,128)(2,1)S(1)} %collective-permute-done.pair_mine), channel_id=1, source_target_pairs={{0,2},{2,0},{1,3},{3,1},{4,6},{6,4},{5,7},{7,5},{8,10},{10,8},{9,1... | collective-permute-start | bytes 1572872 | tf_op jit(solution)/shard_map/ppermute | solution.py:218
  18.1 7.8 %copy-start.1 = (bf16[1024,256]{1,0:T(8,128)(2,1)}, bf16[1024,256]{1,0:T(8,128)(2,1)S(1)}, u32[]{:S(2)}) copy-start(bf16[1024,256]{1,0:T(8,128)(2,1)S(1)} %collective-permute-done.2.next_mine) | copy-start | bytes 1572868
  18.1 19.3 %collective-permute-start.3 = (bf16[1024,256]{1,0:T(8,128)(2,1)S(1)}, bf16[1024,256]{1,0:T(8,128)(2,1)S(1)}, u32[]{:S(2)}, u32[]{:S(2)}) collective-permute-start(bf16[1024,256]{1,0:T(8,128)(2,1)S(1)} %collective-permute-done.2.next_mine), channel_id=1, source_target_pairs={{0,2},{2,0},{1,3},{3,1},{4,6},{6,4},{5,7},{7,5},{8,10},{10,8},{9,1... | collective-permute-start | bytes 1572872 | tf_op jit(solution)/shard_map/ppermute | solution.py:219
  27.1 1.0 %copy-start.8 = (bf16[2,1024,256]{2,1,0:T(8,128)(2,1)}, bf16[2,1024,256]{2,1,0:T(8,128)(2,1)S(1)}, u32[]{:S(2)}) copy-start(bf16[2,1024,256]{2,1,0:T(8,128)(2,1)S(1)} %collective-permute-done.4.other) | copy-start | bytes 3145732
  37.4 0.8 %copy-start.2 = (bf16[1024,256]{1,0:T(8,128)(2,1)}, bf16[1024,256]{1,0:T(8,128)(2,1)S(1)}, u32[]{:S(2)}) copy-start(bf16[1024,256]{1,0:T(8,128)(2,1)S(1)} %collective-permute-done.1.pair_other) | copy-start | bytes 1572868
  38.2 0.9 %copy-start.3 = (bf16[1024,256]{1,0:T(8,128)(2,1)}, bf16[1024,256]{1,0:T(8,128)(2,1)S(1)}, u32[]{:S(2)}) copy-start(bf16[1024,256]{1,0:T(8,128)(2,1)S(1)} %collective-permute-done.3.next_other) | copy-start | bytes 1572868
  49.0 2.1 %collective-permute-start.5 = (f32[512,256]{1,0:T(8,128)}, f32[512,256]{1,0:T(8,128)S(1)}, u32[]{:S(2)}, u32[]{:S(2)}) collective-permute-start(f32[512,256]{1,0:T(8,128)} %get-tuple-element.16), channel_id=1, source_target_pairs={{0,2},{2,0},{1,3},{3,1},{4,6},{6,4},{5,7},{7,5},{8,10},{10,8},{9,1... | collective-permute-start | bytes 1572872 | tf_op jit(solution)/shard_map/ppermute | solution.py:249
  51.1 0.8 %copy-start.4 = (f32[512,256]{1,0:T(8,128)}, f32[512,256]{1,0:T(8,128)S(1)}, u32[]{:S(2)}) copy-start(f32[512,256]{1,0:T(8,128)S(1)} %collective-permute-done.5.other) | copy-start | bytes 1572868
  53.9 7.5 %collective-permute-start.6 = (f32[128,256]{1,0:T(8,128)}, f32[128,256]{1,0:T(8,128)S(1)}, u32[]{:S(2)}, u32[]{:S(2)}) collective-permute-start(f32[128,256]{1,0:T(8,128)} %get-tuple-element.18), channel_id=1, source_target_pairs={{0,4},{4,8},{8,12},{12,0},{1,5},{5,9},{9,13},{13,1},{2,6},{6,10},{... | collective-permute-start | bytes 393224 | tf_op jit(solution)/shard_map/ppermute | solution.py:261
  53.9 17.0 %collective-permute-start.7 = (f32[128,256]{1,0:T(8,128)}, f32[128,256]{1,0:T(8,128)S(1)}, u32[]{:S(2)}, u32[]{:S(2)}) collective-permute-start(f32[128,256]{1,0:T(8,128)} %get-tuple-element.19), channel_id=1, source_target_pairs={{0,8},{4,12},{8,0},{12,4},{1,9},{5,13},{9,1},{13,5},{2,10},{6,14},... | collective-permute-start | bytes 393224 | tf_op jit(solution)/shard_map/ppermute | solution.py:261
  58.7 12.3 %collective-permute-start.8 = (f32[128,256]{1,0:T(8,128)}, f32[128,256]{1,0:T(8,128)S(1)}, u32[]{:S(2)}, u32[]{:S(2)}) collective-permute-start(f32[128,256]{1,0:T(8,128)} %get-tuple-element.20), channel_id=1, source_target_pairs={{0,12},{4,0},{8,4},{12,8},{1,13},{5,1},{9,5},{13,9},{2,14},{6,2},{... | collective-permute-start | bytes 393224 | tf_op jit(solution)/shard_map/ppermute | solution.py:261
  61.4 9.6 %copy-start.5 = (f32[128,256]{1,0:T(8,128)}, f32[128,256]{1,0:T(8,128)S(1)}, u32[]{:S(2)}) copy-start(f32[128,256]{1,0:T(8,128)S(1)} %collective-permute-done.6.refs_1_) | copy-start | bytes 393220
  71.0 0.7 copy-start.6
  71.0 0.7 copy-start.7

commit v2 on v0

v2 whole, which is shorter than its diff:
```python
import functools

import jax
import jax.numpy as jnp
import numpy as np
from jax import lax
from jax.experimental import pallas as pl
from jax.experimental.pallas import tpu as pltpu
from jax.sharding import PartitionSpec as P


JQ = 30
CHUNKS = 1
BF16, F32 = jnp.bfloat16, jnp.float32


def coefficient_table(positions, kblocks):
    total = positions * kblocks
    jsquare = np.float32(JQ * (JQ + 1))
    norm = np.sqrt(jsquare)
    k = (np.arange(total) - total // 2).astype(np.float32)
    same = k / norm
    upper = np.float32(0.5) * np.sqrt(jsquare - k * (k + np.float32(1.0))) / norm
    lower = np.float32(-0.5) * np.sqrt(jsquare - k * (k - np.float32(1.0))) / norm
    rows = []
    for a in range(positions):
        first, last = a * kblocks, a * kblocks + 1
        before = upper[first - 1] if first > 0 else 0.0
        after = lower[last + 1] if last + 1 < total else 0.0
        rows.append([same[first], same[last], lower[last], upper[first], before, after, 0.0, 0.0])
    return np.asarray(rows, np.float32)


def mask_rows(x, count, start):
    row = lax.broadcasted_iota(jnp.int32, x.shape, 0) + start
    return jnp.where(row < count, x.astype(F32), 0.0).astype(x.dtype)


def own_kernel(chunks, block, table, counts, moments, mine, other, *rest):
    outs, rhs = rest[:chunks], rest[chunks]
    position, core = lax.axis_index("ka"), lax.axis_index("vib")
    kblocks, rows, states = mine.shape
    width = states // chunks
    for half, source in ((core, mine), (1 - core, other)):
        start = pl.multiple_of(half * rows, rows)
        for k in range(kblocks):
            live = mask_rows(source[k], counts[k], start)
            for c in range(chunks):
                at = (c * kblocks + k) * width
                rhs[pl.ds(start, rows), at : at + width] = live[:, c * width : (c + 1) * width]

    for v in range(0, rows, block):
        z = jnp.dot(moments[0, v : v + block, :], rhs[...], preferred_element_type=F32)
        x = jnp.dot(moments[1, v : v + block, :], rhs[...], preferred_element_type=F32)
        for c in range(chunks):
            lo, mid, hi = (2 * c) * width, (2 * c + 1) * width, (2 * c + 2) * width
            low = table[position, 0] * z[:, lo:mid] + table[position, 2] * x[:, mid:hi]
            high = table[position, 1] * z[:, mid:hi] + table[position, 3] * x[:, lo:mid]
            outs[c][v : v + block, :width] = low
            outs[c][v : v + block, width:] = high


def halo_kernel(
    places, block, table, counts, moments, pair_mine, pair_other, next_mine, next_other,
    partial, initial, to_other, to_own, rhs, total,
):
    position, core = lax.axis_index("ka"), lax.axis_index("vib")
    parity = lax.rem(position, 2)
    rows, width = pair_mine.shape
    pair_at = pl.multiple_of((1 - parity) * width, width)
    next_at = pl.multiple_of(parity * width, width)
    mine_at = pl.multiple_of(core * rows, rows)
    other_at = pl.multiple_of((1 - core) * rows, rows)
    rhs[pl.ds(mine_at, rows), pl.ds(pair_at, width)] = pair_mine[...]
    rhs[pl.ds(other_at, rows), pl.ds(pair_at, width)] = pair_other[...]
    rhs[pl.ds(mine_at, rows), pl.ds(next_at, width)] = next_mine[...]
    rhs[pl.ds(other_at, rows), pl.ds(next_at, width)] = next_other[...]

    for v in range(0, rows, block):
        x = jnp.dot(moments[1, v : v + block, :], rhs[...], preferred_element_type=F32)
        row = lax.broadcasted_iota(jnp.int32, (block, width), 0) + core * rows + v
        for k in range(2):
            cols = slice(k * width, (k + 1) * width)
            image = partial[v : v + block, cols] + table[position, 4 + k] * x[:, cols]
            image = jnp.where(row < counts[k], image, 0.0)
            high = image.astype(BF16)
            low = (image - high.astype(F32)).astype(BF16)
            both = lax.dot_general(
                initial[k, v : v + block, :],
                jnp.concatenate([high, low], axis=1),
                (((0,), (0,)), ((), ())),
                preferred_element_type=F32,
            )
            both = both[:, :width] + both[:, width:]
            if v == 0 and k == 0:
                total[...] = both
            else:
                total[...] += both

    share = to_own.shape[0] // places
    for s in range(places):
        dest = lax.rem(position + s, places)
        own_at = pl.multiple_of((dest * 2 + core) * share, share)
        other_at = pl.multiple_of((dest * 2 + 1 - core) * share, share)
        to_own[s * share : (s + 1) * share, :] = total[pl.ds(own_at, share), :]
        to_other[s * share : (s + 1) * share, :] = total[pl.ds(other_at, share), :]


def cost(flops, moved):
    return pl.CostEstimate(flops=int(flops), bytes_accessed=int(moved), transcendentals=0)


def kernel_params(mib):
    return pltpu.CompilerParams(vmem_limit_bytes=mib << 20)


def on_device(moments, initial_vectors, final_vectors, basis_counts):
    kblocks, rows, states = initial_vectors.shape
    finals = final_vectors.shape[2]
    whole = moments.shape[2]
    places, cores = lax.axis_size("ka"), lax.axis_size("vib")
    if kblocks != 2 or cores != 2 or places % 2:
        raise ValueError("unsupported mesh")
    chunks = CHUNKS if finals % (CHUNKS * 128) == 0 else 1
    width = finals // chunks
    share = states // (places * cores)
    half = states // cores
    block = 256

    position, core = lax.axis_index("ka"), lax.axis_index("vib")
    parity = position % 2
    table = jnp.asarray(coefficient_table(places, kblocks))
    swap = [(0, 1), (1, 0)]
    pair = [(a, a + 1 - 2 * (a % 2)) for a in range(places)]
    other_side = [(a, min(max(a - 1 + 2 * (a % 2), 0), places - 1)) for a in range(places)]
    smem = pl.BlockSpec(memory_space=pltpu.SMEM)
    vmem = pl.BlockSpec(memory_space=pltpu.VMEM)

    final_other = lax.ppermute(final_vectors, "vib", swap)

    row = core * rows + lax.broadcasted_iota(jnp.int32, (rows, 1), 0)
    halo = []
    for c in range(chunks):
        sides = []
        for k, targets in ((1 - parity, pair), (parity, other_side)):
            block_of = lax.dynamic_slice(
                final_vectors, (k, 0, c * width), (1, rows, width)
            )[0]
            live = row < lax.dynamic_index_in_dim(basis_counts, k, 0, False)
            payload = jnp.where(live, block_of, jnp.zeros((), BF16))
            sides.append(lax.ppermute(payload, "ka", targets))
        halo.append(sides)

    partial = pl.pallas_call(
        functools.partial(own_kernel, chunks, block),
        out_shape=[jax.ShapeDtypeStruct((rows, kblocks * width), F32)] * chunks,
        in_specs=[smem, smem, vmem, vmem, vmem],
        out_specs=[vmem] * chunks,
        scratch_shapes=[pltpu.VMEM((whole, kblocks * finals), BF16)],
        cost_estimate=cost(
            4 * rows * whole * kblocks * finals, 2 * moments.size + 8 * rows * finals
        ),
        compiler_params=kernel_params(20),
        name="own",
    )(table, basis_counts, moments, final_vectors, final_other)

    blocks = []
    for c in range(chunks):
        near, far = halo[c]
        near_other = lax.ppermute(near, "vib", swap)
        far_other = lax.ppermute(far, "vib", swap)
        to_other, to_own = pl.pallas_call(
            functools.partial(halo_kernel, places, block),
            out_shape=[jax.ShapeDtypeStruct((half, width), F32)] * 2,
            in_specs=[smem, smem] + [vmem] * 7,
            out_specs=[vmem] * 2,
            scratch_shapes=[
                pltpu.VMEM((whole, kblocks * width), BF16),
                pltpu.VMEM((states, width), F32),
            ],
            cost_estimate=cost(
                2 * rows * whole * kblocks * width + 8 * rows * states * width,
                moments.size + 4 * rows * states,
            ),
            compiler_params=kernel_params(20),
            name="halo",
        )(
            table, basis_counts, moments, near, near_other, far, far_other,
            partial[c], initial_vectors,
        )
        received = lax.ppermute(to_other, "vib", swap)
        sums = (to_own + received).reshape(places, share, width)
        terms = [sums[0]]
        for s in range(1, places):
            turn = [(a, (a + s) % places) for a in range(places)]
            terms.append(lax.ppermute(sums[s], "ka", turn))
        blocks.append(terms)

    columns = []
    for terms in blocks:
        amplitude = terms[0]
        for term in terms[1:]:
            amplitude = amplitude + term
        columns.append(amplitude * amplitude)
    return jnp.concatenate(columns, axis=1)


def solution(mesh):
    in_specs = (
        P(None, "vib", None),
        P("ka", "vib", "grp"),
        P("ka", "vib", ("grp", "fin")),
        P(("grp", "ka")),
    )
    out_specs = P(("grp", "ka", "vib"), "fin")

    return jax.shard_map(
        on_device, mesh=mesh, in_specs=in_specs, out_specs=out_specs, check_vma=False
    )
```

time: 142 us -> 60 us (0.42)
  waiting for transfers between devices: 97.5 us -> 25.6 us
  matrix products: 17.5 us -> 0 us
  between operations: 13.5 us -> 0.09 us
  Pallas kernels: 0 us -> 11.7 us
  starting transfers between devices: 5.98 us -> 11.1 us
  local copies, waits for them, and re-layouts: 4.75 us -> 7.37 us
    psum x1 -> x0, waiting for transfers between devices: 58.5 us -> none  [on_device(): summed = lax.psum(amplitude, ('ka', 'vib'))]
    dot_general x2 -> x0, matrix products: 17.5 us -> none  [the longest x1 9.88 us: on_device(): jnp.einsum('kvi,vkf->if', initial_live.astype(jnp.float32), combined, pre...]
    all_gather x1 -> x0, waiting for transfers between devices: 13.4 us -> none  [on_device(): final_whole = lax.all_gather(final_live, 'vib', axis=1, tiled=True)]
    pallas_call x0 -> x2, Pallas kernels: none -> 11.7 us  [the longest x1 6.19 us: on_device(): pl.pallas_call(functools.partial(halo_kernel, places, block), out_shape=[...]
    ppermute x2 -> x9, starting transfers between devices: 5.93 us -> 11.1 us  [the longest x2 6.11 us: on_device(): sides.append(lax.ppermute(payload, 'ka', targets))]
    unnamed x5 -> x10, local copies, waits for them, and re-layouts: 3.29 us -> 5.94 us
    ppermute x2 -> x9, waiting for transfers between devices: 25.6 us -> 25.6 us  [the longest x2 12.3 us: on_device(): sides.append(lax.ppermute(payload, 'ka', targets))]
  transfers between devices with their start and end apart: 4 -> 9, of which waited for: 4 -> 5; matrix products, arithmetic and copies ran while one was open for 0% -> 8% of each run, Pallas kernels for 0% -> 9%
where the time goes in v2:
time: 60 us; the launch traced here: 59.8 us
  waiting for transfers between devices  25.6 us (43%)
  Pallas kernels  11.7 us (20%)
  starting transfers between devices  11.1 us (18%)
  local copies, waits for them, and re-layouts  7.37 us (12%)
  other arithmetic  3.86 us (6%)
    ppermute x2, waiting for transfers between devices, on_device(): sides.append(lax.ppermute(payload, 'ka', targets))  12.3 us
    ppermute x3, waiting for transfers between devices, on_device(): terms.append(lax.ppermute(sums[s], 'ka', turn))  11.7 us
    pallas_call x1, Pallas kernels, on_device(): pl.pallas_call(functools.partial(halo_kernel, places, block), out_shape=[...  6.19 us
    ppermute x2, starting transfers between devices, on_device(): sides.append(lax.ppermute(payload, 'ka', targets))  6.11 us
    unnamed x10, local copies, waits for them, and re-layouts  5.94 us
    pallas_call x1, Pallas kernels, on_device(): pl.pallas_call(functools.partial(own_kernel, chunks, block), out_shape=[j...  5.54 us
    ppermute x3, starting transfers between devices, on_device(): terms.append(lax.ppermute(sums[s], 'ka', turn))  3.88 us
    select_n x1, other arithmetic, on_device(): payload = jnp.where(live, block_of, jnp.zeros((), BF16))  1.77 us
  transfers between devices with their start and end apart: 9, of which 5 were waited for; matrix products, arithmetic and copies ran while one was open for 8% of the time, Pallas kernels for 9%

profile of v2, /device:TPU:0, one launch (start us, length us, event | category | flops | bytes accessed | tf_op | source)
XLA Modules:
  0.0 59.8 jit_solution(12285526815854067626)
XLA Ops:
  0.0 0.5 collective-permute-start.4
  0.5 1.4 %fusion.6 = (s32[1]{0:T(128)}, s32[1]{0:T(128)}) fusion(s32[2]{0:T(128)} %counts.3, s32[]{:T(128)S(6)} %select_n.26, s32[]{:T(128)S(6)} %select_n.24), kind=kLoop, calls=%fused_computation.10 | loop fusion | bytes 24 | tf_op jit(solution)/shard_map/jit(dynamic_index_in_dim)/dynamic_slice | solution.py:149
  1.9 1.3 %fusion.3 = (pred[1024]{0:T(1024)(128)(4,1)S(1)}, pred[1024]{0:T(1024)(128)(4,1)S(1)}) fusion(s32[]{:T(128)} %bitcast.2, s32[]{:T(128)S(6)} %mul.6, s32[]{:T(128)} %bitcast), kind=kLoop, calls=%fused_computation.7 | loop fusion | flops 3072 | bytes 2060 | tf_op jit(solution)/shard_map/lt | solution.py:149
  3.2 1.8 %bitcast_select_fusion = (bf16[1024,256]{1,0:T(8,128)(2,1)S(1)}, bf16[1024,256]{1,0:T(8,128)(2,1)S(1)}) fusion(bf16[2,1024,256]{2,1,0:T(8,128)(2,1)} %mine.1, s32[]{:T(128)S(6)} %select_n.26, pred[1024]{0:T(1024)(128)(4,1)S(1)} %get-tuple-element.16, s32[]{:T(128)S(6)} %select_n.24, pred[1024]{0:T(1024)(128)(4,1)S(1)} %get-tuple-element.17), kind=kLoop, calls=%fused_computation | loop fusion | flops 524288 | bytes 2099208 | tf_op jit(solution)/shard_map/jit(_where)/select_n | solution.py:150
  5.0 0.7 %collective-permute-start.2 = (bf16[1024,256]{1,0:T(8,128)(2,1)S(1)}, bf16[1024,256]{1,0:T(8,128)(2,1)S(1)}, u32[]{:S(2)}, u32[]{:S(2)}) collective-permute-start(bf16[1024,256]{1,0:T(8,128)(2,1)S(1)} %get-tuple-element.9), channel_id=1, source_target_pairs={{0,0},{4,8},{8,4},{12,12},{1,1},{5,9},{9,5},{13,13},{2,2},{6,10},{... | collective-permute-start | bytes 1572872 | tf_op jit(solution)/shard_map/ppermute | solution.py:151
  5.7 5.4 %collective-permute-start = (bf16[1024,256]{1,0:T(8,128)(2,1)S(1)}, bf16[1024,256]{1,0:T(8,128)(2,1)S(1)}, u32[]{:S(2)}, u32[]{:S(2)}) collective-permute-start(bf16[1024,256]{1,0:T(8,128)(2,1)S(1)} %get-tuple-element.10), channel_id=1, source_target_pairs={{0,4},{4,0},{8,12},{12,8},{1,5},{5,1},{9,13},{13,9},{2,6},{6,2},{1... | collective-permute-start | bytes 1572872 | tf_op jit(solution)/shard_map/ppermute | solution.py:151
  11.1 0.0 collective-permute-done.2.next_mine
  11.1 0.0 collective-permute-start.3
  11.1 12.3 %collective-permute-done.pair_mine = bf16[1024,256]{1,0:T(8,128)(2,1)S(1)} collective-permute-done((bf16[1024,256]{1,0:T(8,128)(2,1)S(1)}, bf16[1024,256]{1,0:T(8,128)(2,1)S(1)}, u32[]{:S(2)}, u32[]{:S(2)}) %collective-permute-start) | collective-permute-done | bytes 524320 | tf_op jit(solution)/shard_map/ppermute | solution.py:151
  23.4 0.0 collective-permute-start.1
  23.4 0.0 collective-permute-done.4.other
  23.5 0.0 copy-start
  23.5 3.4 %copy-done = bf16[2,1024,2048]{2,1,0:T(8,128)(2,1)S(1)} copy-done((bf16[2,1024,2048]{2,1,0:T(8,128)(2,1)S(1)}, bf16[2,1024,2048]{2,1,0:T(8,128)(2,1)}, u32[]{:S(2)}) %copy-start) | copy-done | bytes 8388632
  26.8 0.0 copy-start.2
  26.8 1.2 %copy-done.2 = bf16[2,1024,256]{2,1,0:T(8,128)(2,1)S(1)} copy-done((bf16[2,1024,256]{2,1,0:T(8,128)(2,1)S(1)}, bf16[2,1024,256]{2,1,0:T(8,128)(2,1)}, u32[]{:S(2)}) %copy-start.2) | copy-done | bytes 1048600
  28.1 0.0 copy-start.3
  28.1 0.7 %copy-done.3 = s32[2]{0:T(128)S(1)} copy-done((s32[2]{0:T(128)S(1)}, s32[2]{0:T(128)}, u32[]{:S(2)}) %copy-start.3) | copy-done | bytes 32
  28.7 0.0 copy-start.4
  28.7 0.7 %copy-done.4 = f32[4,8]{1,0:T(4,128)S(1)} copy-done((f32[4,8]{1,0:T(4,128)S(1)}, f32[4,8]{1,0:T(4,128)}, u32[]{:S(2)}) %copy-start.4) | copy-done | bytes 152
  29.4 0.0 copy-start.1
  29.4 5.5 %own.1.partial = f32[1024,512]{1,0:T(8,128)S(1)} custom-call(f32[4,8]{1,0:T(4,128)S(1)} %copy-done.4, s32[2]{0:T(128)S(1)} %copy-done.3, bf16[2,1024,2048]{2,1,0:T(8,128)(2,1)S(1)} %copy-done, bf16[2,1024,256]{2,1,0:T(8,128)(2,1)S(1)} %copy-done.2, bf16[2,1024,256]{2,1,0:T(8,128)(2,1)S(1)} %collective-permute-done.4.other), custom_call_target="tpu_custom_call" | custom-call | flops 4294967296 | bytes 10485760 | tf_op jit(solution)/shard_map/own/pallas_call | solution.py:154
  34.9 0.0 collective-permute-done.3.next_other
  35.0 0.0 collective-permute-done.1.pair_other
  35.0 0.0 copy-done.1
  35.0 6.2 %halo.1 = (f32[512,256]{1,0:T(8,128)S(1)}, f32[512,256]{1,0:T(8,128)S(1)}) custom-call(f32[4,8]{1,0:T(4,128)S(1)} %copy-done.4, s32[2]{0:T(128)S(1)} %copy-done.3, bf16[2,1024,2048]{2,1,0:T(8,128)(2,1)S(1)} %copy-done, bf16[1024,256]{1,0:T(8,128)(2,1)S(1)} %collective-permute-done.pair_mine, bf16[1024,256]{1,0:T(8,128)(2,1)S(1)} %collective-permute-done.1.pair_other, ...), custom_call_target="tpu_custom_call" | custom-call | flops 4294967296 | bytes 8388608 | tf_op jit(solution)/shard_map/halo/pallas_call | solution.py:172
  41.2 0.6 %collective-permute-start.5 = (f32[512,256]{1,0:T(8,128)S(1)}, f32[512,256]{1,0:T(8,128)S(1)}, u32[]{:S(2)}, u32[]{:S(2)}) collective-permute-start(f32[512,256]{1,0:T(8,128)S(1)} %get-tuple-element.8), channel_id=1, source_target_pairs={{0,2},{2,0},{1,3},{3,1},{4,6},{6,4},{5,7},{7,5},{8,10},{10,8},{9,1... | collective-permute-start | bytes 1572872 | tf_op jit(solution)/shard_map/ppermute | solution.py:191
  41.8 1.5 %collective-permute-done.5 = f32[512,256]{1,0:T(8,128)S(1)} collective-permute-done((f32[512,256]{1,0:T(8,128)S(1)}, f32[512,256]{1,0:T(8,128)S(1)}, u32[]{:S(2)}, u32[]{:S(2)}) %collective-permute-start.5) | collective-permute-done | bytes 524320 | tf_op jit(solution)/shard_map/ppermute | solution.py:191
  43.4 0.1 add.45
  43.5 1.8 %collective-permute-start.6 = (f32[128,256]{1,0:T(8,128)S(1)}, f32[128,256]{1,0:T(8,128)S(1)}, u32[]{:S(2)}, u32[]{:S(2)}) collective-permute-start(f32[128,256]{1,0:T(8,128)S(1)} %get-tuple-element.11), channel_id=1, source_target_pairs={{0,4},{4,8},{8,12},{12,0},{1,5},{5,9},{9,13},{13,1},{2,6},{6,10},{... | collective-permute-start | bytes 393224 | tf_op jit(solution)/shard_map/ppermute | solution.py:196
  45.3 2.1 %collective-permute-start.8 = (f32[128,256]{1,0:T(8,128)S(1)}, f32[128,256]{1,0:T(8,128)S(1)}, u32[]{:S(2)}, u32[]{:S(2)}) collective-permute-start(f32[128,256]{1,0:T(8,128)S(1)} %get-tuple-element.12), channel_id=1, source_target_pairs={{0,12},{4,0},{8,4},{12,8},{1,13},{5,1},{9,5},{13,9},{2,14},{6,2},{... | collective-permute-start | bytes 393224 | tf_op jit(solution)/shard_map/ppermute | solution.py:196
  47.3 0.0 collective-permute-start.7
  47.3 4.4 %collective-permute-done.6 = f32[128,256]{1,0:T(8,128)S(1)} collective-permute-done((f32[128,256]{1,0:T(8,128)S(1)}, f32[128,256]{1,0:T(8,128)S(1)}, u32[]{:S(2)}, u32[]{:S(2)}) %collective-permute-start.6) | collective-permute-done | bytes 131104 | tf_op jit(solution)/shard_map/ppermute | solution.py:196
  51.7 2.2 %collective-permute-done.8 = f32[128,256]{1,0:T(8,128)S(1)} collective-permute-done((f32[128,256]{1,0:T(8,128)S(1)}, f32[128,256]{1,0:T(8,128)S(1)}, u32[]{:S(2)}, u32[]{:S(2)}) %collective-permute-start.8) | collective-permute-done | bytes 131104 | tf_op jit(solution)/shard_map/ppermute | solution.py:196
  53.9 5.1 %collective-permute-done.7 = f32[128,256]{1,0:T(8,128)S(1)} collective-permute-done((f32[128,256]{1,0:T(8,128)S(1)}, f32[128,256]{1,0:T(8,128)S(1)}, u32[]{:S(2)}, u32[]{:S(2)}) %collective-permute-start.7) | collective-permute-done | bytes 131104 | tf_op jit(solution)/shard_map/ppermute | solution.py:196
  59.1 0.7 %fusion.2 = f32[128,256]{1,0:T(8,128)} fusion(f32[128,256]{1,0:T(8,128)S(1)} %collective-permute-done.8, f32[128,256]{1,0:T(8,128)S(1)} %collective-permute-done.7, f32[128,256]{1,0:T(8,128)S(1)} %collective-permute-done.6, f32[512,256]{1,0:T(8,128)S(1)} %add.45), kind=kLoop, calls=%fused_computation.5 | loop fusion | flops 131072 | bytes 655360 | tf_op jit(solution)/shard_map/mul | solution.py:204
  (1 shorter events, 0.0 us)
Async XLA Ops:
  0.0 23.5 %collective-permute-start.4 = (bf16[2,1024,256]{2,1,0:T(8,128)(2,1)}, bf16[2,1024,256]{2,1,0:T(8,128)(2,1)S(1)}, u32[]{:S(2)}, u32[]{:S(2)}) collective-permute-start(bf16[2,1024,256]{2,1,0:T(8,128)(2,1)} %mine.1), channel_id=1, source_target_pairs={{0,2},{2,0},{1,3},{3,1},{4,6},{6,4},{5,7},{7,5},{8,10},{10,8},{9,1... | collective-permute-start | bytes 3145736 | tf_op jit(solution)/shard_map/ppermute | solution.py:139
  5.0 6.1 %collective-permute-start.2 = (bf16[1024,256]{1,0:T(8,128)(2,1)S(1)}, bf16[1024,256]{1,0:T(8,128)(2,1)S(1)}, u32[]{:S(2)}, u32[]{:S(2)}) collective-permute-start(bf16[1024,256]{1,0:T(8,128)(2,1)S(1)} %get-tuple-element.9), channel_id=1, source_target_pairs={{0,0},{4,8},{8,4},{12,12},{1,1},{5,9},{9,5},{13,13},{2,2},{6,10},{... | collective-permute-start | bytes 1572872 | tf_op jit(solution)/shard_map/ppermute | solution.py:151
  5.7 17.7 %collective-permute-start = (bf16[1024,256]{1,0:T(8,128)(2,1)S(1)}, bf16[1024,256]{1,0:T(8,128)(2,1)S(1)}, u32[]{:S(2)}, u32[]{:S(2)}) collective-permute-start(bf16[1024,256]{1,0:T(8,128)(2,1)S(1)} %get-tuple-element.10), channel_id=1, source_target_pairs={{0,4},{4,0},{8,12},{12,8},{1,5},{5,1},{9,13},{13,9},{2,6},{6,2},{1... | collective-permute-start | bytes 1572872 | tf_op jit(solution)/shard_map/ppermute | solution.py:151
  11.1 23.8 %collective-permute-start.3 = (bf16[1024,256]{1,0:T(8,128)(2,1)S(1)}, bf16[1024,256]{1,0:T(8,128)(2,1)S(1)}, u32[]{:S(2)}, u32[]{:S(2)}) collective-permute-start(bf16[1024,256]{1,0:T(8,128)(2,1)S(1)} %collective-permute-done.2.next_mine), channel_id=1, source_target_pairs={{0,2},{2,0},{1,3},{3,1},{4,6},{6,4},{5,7},{7,5},{8,10},{10,8},{9,1... | collective-permute-start | bytes 1572872 | tf_op jit(solution)/shard_map/ppermute | solution.py:171
  23.4 11.5 %collective-permute-start.1 = (bf16[1024,256]{1,0:T(8,128)(2,1)S(1)}, bf16[1024,256]{1,0:T(8,128)(2,1)S(1)}, u32[]{:S(2)}, u32[]{:S(2)}) collective-permute-start(bf16[1024,256]{1,0:T(8,128)(2,1)S(1)} %collective-permute-done.pair_mine), channel_id=1, source_target_pairs={{0,2},{2,0},{1,3},{3,1},{4,6},{6,4},{5,7},{7,5},{8,10},{10,8},{9,1... | collective-permute-start | bytes 1572872 | tf_op jit(solution)/shard_map/ppermute | solution.py:170
  23.5 3.4 %copy-start = (bf16[2,1024,2048]{2,1,0:T(8,128)(2,1)S(1)}, bf16[2,1024,2048]{2,1,0:T(8,128)(2,1)}, u32[]{:S(2)}) copy-start(bf16[2,1024,2048]{2,1,0:T(8,128)(2,1)} %moments.3) | copy-start | bytes 25165828
  26.8 1.2 %copy-start.2 = (bf16[2,1024,256]{2,1,0:T(8,128)(2,1)S(1)}, bf16[2,1024,256]{2,1,0:T(8,128)(2,1)}, u32[]{:S(2)}) copy-start(bf16[2,1024,256]{2,1,0:T(8,128)(2,1)} %mine.1) | copy-start | bytes 3145732
  28.1 0.7 %copy-start.3 = (s32[2]{0:T(128)S(1)}, s32[2]{0:T(128)}, u32[]{:S(2)}) copy-start(s32[2]{0:T(128)} %counts.3) | copy-start | bytes 28
  28.7 0.7 %copy-start.4 = (f32[4,8]{1,0:T(4,128)S(1)}, f32[4,8]{1,0:T(4,128)}, u32[]{:S(2)}) copy-start(f32[4,8]{1,0:T(4,128)} %constant.38.clone.table) | copy-start | bytes 388
  29.4 5.6 %copy-start.1 = (bf16[2,1024,1024]{2,1,0:T(8,128)(2,1)S(1)}, bf16[2,1024,1024]{2,1,0:T(8,128)(2,1)}, u32[]{:S(2)}) copy-start(bf16[2,1024,1024]{2,1,0:T(8,128)(2,1)} %initial.1) | copy-start | bytes 12582916
  41.2 2.2 %collective-permute-start.5 = (f32[512,256]{1,0:T(8,128)S(1)}, f32[512,256]{1,0:T(8,128)S(1)}, u32[]{:S(2)}, u32[]{:S(2)}) collective-permute-start(f32[512,256]{1,0:T(8,128)S(1)} %get-tuple-element.8), channel_id=1, source_target_pairs={{0,2},{2,0},{1,3},{3,1},{4,6},{6,4},{5,7},{7,5},{8,10},{10,8},{9,1... | collective-permute-start | bytes 1572872 | tf_op jit(solution)/shard_map/ppermute | solution.py:191
  43.5 8.3 %collective-permute-start.6 = (f32[128,256]{1,0:T(8,128)S(1)}, f32[128,256]{1,0:T(8,128)S(1)}, u32[]{:S(2)}, u32[]{:S(2)}) collective-permute-start(f32[128,256]{1,0:T(8,128)S(1)} %get-tuple-element.11), channel_id=1, source_target_pairs={{0,4},{4,8},{8,12},{12,0},{1,5},{5,9},{9,13},{13,1},{2,6},{6,10},{... | collective-permute-start | bytes 393224 | tf_op jit(solution)/shard_map/ppermute | solution.py:196
  45.3 8.7 %collective-permute-start.8 = (f32[128,256]{1,0:T(8,128)S(1)}, f32[128,256]{1,0:T(8,128)S(1)}, u32[]{:S(2)}, u32[]{:S(2)}) collective-permute-start(f32[128,256]{1,0:T(8,128)S(1)} %get-tuple-element.12), channel_id=1, source_target_pairs={{0,12},{4,0},{8,4},{12,8},{1,13},{5,1},{9,5},{13,9},{2,14},{6,2},{... | collective-permute-start | bytes 393224 | tf_op jit(solution)/shard_map/ppermute | solution.py:196
  47.3 11.7 %collective-permute-start.7 = (f32[128,256]{1,0:T(8,128)S(1)}, f32[128,256]{1,0:T(8,128)S(1)}, u32[]{:S(2)}, u32[]{:S(2)}) collective-permute-start(f32[128,256]{1,0:T(8,128)S(1)} %get-tuple-element.13), channel_id=1, source_target_pairs={{0,8},{4,12},{8,0},{12,4},{1,9},{5,13},{9,1},{13,5},{2,10},{6,14},... | collective-permute-start | bytes 393224 | tf_op jit(solution)/shard_map/ppermute | solution.py:196

commit v3 on v2

v3 whole, which is shorter than its diff:
```python
import functools

import jax
import jax.numpy as jnp
from jax import lax
from jax.experimental import pallas as pl
from jax.experimental.pallas import tpu as pltpu
from jax.sharding import PartitionSpec as P


JQ = 30
CHUNKS = 1
BF16, F32 = jnp.bfloat16, jnp.float32


def couplings(position, kblocks, width):
    total = lax.axis_size("ka") * kblocks
    jsquare = float(JQ * (JQ + 1))
    norm = jnp.sqrt(jnp.full((1, width), jsquare, F32))

    def k_value(k):
        return jnp.full((1, width), (k - total // 2).astype(F32), F32)

    first = position * kblocks
    rows = []
    for j in range(kblocks):
        k = first + j
        here, under, over = k_value(k), k_value(k - 1), k_value(k + 1)
        upper = 0.5 * jnp.sqrt(jnp.maximum(jsquare - under * (under + 1.0), 0.0)) / norm
        lower = -0.5 * jnp.sqrt(jnp.maximum(jsquare - over * (over - 1.0), 0.0)) / norm
        upper = jnp.where(k > 0, upper, 0.0)
        lower = jnp.where(k < total - 1, lower, 0.0)
        rows.append((here / norm, upper, lower))
    return rows


def keep_rows(x, count, start):
    row = lax.broadcasted_iota(jnp.int32, x.shape, 0) + start
    return jnp.where(row < count, x.astype(F32), 0.0).astype(x.dtype)


def pack_kernel(chunks, counts, final, *rest):
    outs, (held, live, sems) = rest[: 2 * chunks], rest[2 * chunks :]
    position, core = lax.axis_index("ka"), lax.axis_index("vib")
    parity = lax.rem(position, 2)
    rows, states = held.shape[1:]
    width = states // chunks
    sizes = pltpu.make_async_copy(counts, live, sems.at[2])
    sizes.start()
    copies = []
    for slot, k in enumerate((1 - parity, parity)):
        copies.append(pltpu.make_async_copy(final.at[k], held.at[slot], sems.at[slot]))
        copies[-1].start()
    sizes.wait()
    for slot, k in enumerate((1 - parity, parity)):
        copies[slot].wait()
        for c in range(chunks):
            block = held[slot, :, c * width : (c + 1) * width]
            outs[2 * c + slot][...] = keep_rows(block, live[k], core * rows)


def own_kernel(chunks, block, counts, moments, other, *rest):
    payload, outs = rest[: 2 * chunks], rest[2 * chunks : 3 * chunks]
    cross, rhs, direct, live, sems = rest[3 * chunks :]
    position, core = lax.axis_index("ka"), lax.axis_index("vib")
    parity = lax.rem(position, 2)
    kblocks, rows, states = other.shape
    width = states // chunks
    steps = rows // block
    sizes = pltpu.make_async_copy(counts, live, sems.at[2 * steps])
    sizes.start()
    copies = []
    for s in range(steps):
        at = pl.ds(s * block, block)
        for m, target in ((0, direct), (1, cross)):
            copies.append(
                pltpu.make_async_copy(moments.at[m, at], target.at[at], sems.at[2 * s + m])
            )
            copies[-1].start()
    mine_at = pl.multiple_of(core * rows, rows)
    other_at = pl.multiple_of((1 - core) * rows, rows)
    for c in range(chunks):
        for slot, k in enumerate((1 - parity, parity)):
            at = pl.multiple_of((c * kblocks + k) * width, width)
            rhs[pl.ds(mine_at, rows), pl.ds(at, width)] = payload[2 * c + slot][...]
    sizes.wait()
    for k in range(kblocks):
        block_of = keep_rows(other[k], live[k], other_at)
        for c in range(chunks):
            at = (c * kblocks + k) * width
            rhs[pl.ds(other_at, rows), at : at + width] = block_of[:, c * width : (c + 1) * width]

    (same_low, _, lower), (same_high, upper, _) = couplings(position, kblocks, width)
    for s in range(steps):
        v = slice(s * block, (s + 1) * block)
        copies[2 * s].wait()
        z = jnp.dot(direct[v, :], rhs[...], preferred_element_type=F32)
        copies[2 * s + 1].wait()
        x = jnp.dot(cross[v, :], rhs[...], preferred_element_type=F32)
        for c in range(chunks):
            lo, mid, hi = (2 * c) * width, (2 * c + 1) * width, (2 * c + 2) * width
            outs[c][v, :width] = same_low * z[:, lo:mid] + lower * x[:, mid:hi]
            outs[c][v, width:] = same_high * z[:, mid:hi] + upper * x[:, lo:mid]


def halo_kernel(
    places, block, counts, cross, pair_mine, pair_other, next_mine, next_other,
    partial, initial, to_other, to_own, rhs, images, total, live, sems,
):
    sizes = pltpu.make_async_copy(counts, live, sems.at[0])
    sizes.start()
    position, core = lax.axis_index("ka"), lax.axis_index("vib")
    parity = lax.rem(position, 2)
    rows, width = pair_mine.shape
    states = initial.shape[2]
    pair_at = pl.multiple_of((1 - parity) * width, width)
    next_at = pl.multiple_of(parity * width, width)
    mine_at = pl.multiple_of(core * rows, rows)
    other_at = pl.multiple_of((1 - core) * rows, rows)
    rhs[pl.ds(mine_at, rows), pl.ds(pair_at, width)] = pair_mine[...]
    rhs[pl.ds(other_at, rows), pl.ds(pair_at, width)] = pair_other[...]
    rhs[pl.ds(mine_at, rows), pl.ds(next_at, width)] = next_mine[...]
    rhs[pl.ds(other_at, rows), pl.ds(next_at, width)] = next_other[...]
    (_, upper, _), (_, _, lower) = couplings(position, 2, width)
    sizes.wait()

    for v in range(0, rows, block):
        x = jnp.dot(cross[v : v + block, :], rhs[...], preferred_element_type=F32)
        row = lax.broadcasted_iota(jnp.int32, (block, width), 0) + core * rows + v
        for k, weight in ((0, upper), (1, lower)):
            cols = slice(k * width, (k + 1) * width)
            image = partial[v : v + block, cols] + weight * x[:, cols]
            image = jnp.where(row < live[k], image, 0.0)
            high = image.astype(BF16)
            images[k * rows + v : k * rows + v + block, :width] = high
            images[k * rows + v : k * rows + v + block, width:] = (
                image - high.astype(F32)
            ).astype(BF16)

    vectors = initial.reshape(2 * rows, states)
    for i in range(0, states, block):
        both = lax.dot_general(
            vectors[:, i : i + block],
            images[...],
            (((0,), (0,)), ((), ())),
            preferred_element_type=F32,
        )
        total[i : i + block, :] = both[:, :width] + both[:, width:]

    share = to_own.shape[0] // places
    for s in range(places):
        dest = lax.rem(position + s, places)
        own_at = pl.multiple_of((dest * 2 + core) * share, share)
        other_at = pl.multiple_of((dest * 2 + 1 - core) * share, share)
        to_own[s * share : (s + 1) * share, :] = total[pl.ds(own_at, share), :]
        to_other[s * share : (s + 1) * share, :] = total[pl.ds(other_at, share), :]


def cost(flops, moved):
    return pl.CostEstimate(flops=int(flops), bytes_accessed=int(moved), transcendentals=0)


def kernel_params(mib):
    return pltpu.CompilerParams(vmem_limit_bytes=mib << 20)


def on_device(moments, initial_vectors, final_vectors, basis_counts):
    kblocks, rows, states = initial_vectors.shape
    finals = final_vectors.shape[2]
    whole = moments.shape[2]
    places, cores = lax.axis_size("ka"), lax.axis_size("vib")
    if kblocks != 2 or cores != 2 or places % 2:
        raise ValueError("unsupported mesh")
    chunks = CHUNKS if finals % (CHUNKS * 128) == 0 else 1
    width = finals // chunks
    share = states // (places * cores)
    half = states // cores
    block = 256

    def resting(x):
        return pltpu.with_memory_space_constraint(x, pltpu.HBM)

    swap = [(0, 1), (1, 0)]
    pair = [(a, a + 1 - 2 * (a % 2)) for a in range(places)]
    other_side = [(a, min(max(a - 1 + 2 * (a % 2), 0), places - 1)) for a in range(places)]
    vmem = pl.BlockSpec(memory_space=pltpu.VMEM)
    hbm = pl.BlockSpec(memory_space=pltpu.HBM)
    counted = pltpu.SMEM((kblocks,), jnp.int32)

    payload = pl.pallas_call(
        functools.partial(pack_kernel, chunks),
        out_shape=[jax.ShapeDtypeStruct((rows, width), BF16)] * (2 * chunks),
        in_specs=[hbm, hbm],
        out_specs=[vmem] * (2 * chunks),
        scratch_shapes=[
            pltpu.VMEM((kblocks, rows, finals), BF16),
            counted,
            pltpu.SemaphoreType.DMA((3,)),
        ],
        cost_estimate=cost(0, 4 * kblocks * rows * finals),
        compiler_params=kernel_params(8),
        name="pack",
    )(resting(basis_counts), resting(final_vectors))

    halo = []
    for c in range(chunks):
        near = lax.ppermute(payload[2 * c], "ka", pair)
        far = lax.ppermute(payload[2 * c + 1], "ka", other_side)
        halo.append((near, far))
    final_other = lax.ppermute(final_vectors, "vib", swap)

    *partial, cross = pl.pallas_call(
        functools.partial(own_kernel, chunks, block),
        out_shape=[jax.ShapeDtypeStruct((rows, kblocks * width), F32)] * chunks
        + [jax.ShapeDtypeStruct((rows, whole), BF16)],
        in_specs=[hbm, hbm] + [vmem] * (1 + 2 * chunks),
        out_specs=[vmem] * (chunks + 1),
        scratch_shapes=[
            pltpu.VMEM((whole, kblocks * finals), BF16),
            pltpu.VMEM((rows, whole), BF16),
            counted,
            pltpu.SemaphoreType.DMA((2 * (rows // block) + 1,)),
        ],
        cost_estimate=cost(
            4 * rows * whole * kblocks * finals, 2 * moments.size + 8 * rows * finals
        ),
        compiler_params=kernel_params(20),
        name="own",
    )(resting(basis_counts), resting(moments), final_other, *payload)

    blocks = []
    for c in range(chunks):
        near, far = halo[c]
        near_other = lax.ppermute(near, "vib", swap)
        far_other = lax.ppermute(far, "vib", swap)
        to_other, to_own = pl.pallas_call(
            functools.partial(halo_kernel, places, block),
            out_shape=[jax.ShapeDtypeStruct((half, width), F32)] * 2,
            in_specs=[hbm] + [vmem] * 7,
            out_specs=[vmem] * 2,
            scratch_shapes=[
                pltpu.VMEM((whole, kblocks * width), BF16),
                pltpu.VMEM((kblocks * rows, 2 * width), BF16),
                pltpu.VMEM((states, width), F32),
                counted,
                pltpu.SemaphoreType.DMA((1,)),
            ],
            cost_estimate=cost(
                2 * rows * whole * kblocks * width + 8 * rows * states * width,
                moments.size + 4 * rows * states,
            ),
            compiler_params=kernel_params(20),
            name="halo",
        )(
            resting(basis_counts), cross, near, near_other, far, far_other, partial[c],
            initial_vectors,
        )
        received = lax.ppermute(to_other, "vib", swap)
        sums = (to_own + received).reshape(places, share, width)
        terms = [sums[0]]
        for s in range(1, places):
            turn = [(a, (a + s) % places) for a in range(places)]
            terms.append(lax.ppermute(sums[s], "ka", turn))
        blocks.append(terms)

    columns = []
    for terms in blocks:
        amplitude = terms[0]
        for term in terms[1:]:
            amplitude = amplitude + term
        columns.append(amplitude * amplitude)
    return jnp.concatenate(columns, axis=1)


def solution(mesh):
    in_specs = (
        P(None, "vib", None),
        P("ka", "vib", "grp"),
        P("ka", "vib", ("grp", "fin")),
        P(("grp", "ka")),
    )
    out_specs = P(("grp", "ka", "vib"), "fin")

    return jax.shard_map(
        on_device, mesh=mesh, in_specs=in_specs, out_specs=out_specs, check_vma=False
    )
```

time: 60 us -> 48.9 us (0.81)
  the two profiles are of different devices: /device:TPU:0 before, /device:TPU:30 now
where the time goes in v3:
time: 48.9 us; the launch traced here: 48.8 us
  waiting for transfers between devices  26.9 us (55%)
  Pallas kernels  13.8 us (28%)
  starting transfers between devices  7.23 us (15%)
  other arithmetic  0.76 us (2%)
    ppermute x1, waiting for transfers between devices, on_device(): near = lax.ppermute(payload[2 * c], 'ka', pair)  13.1 us
    ppermute x3, waiting for transfers between devices, on_device(): terms.append(lax.ppermute(sums[s], 'ka', turn))  11.9 us
    pallas_call x1, Pallas kernels, on_device(): pl.pallas_call(functools.partial(own_kernel, chunks, block), out_shape=[j...  6.97 us
    pallas_call x1, Pallas kernels, on_device(): pl.pallas_call(functools.partial(halo_kernel, places, block), out_shape=[...  5.49 us
    ppermute x3, starting transfers between devices, on_device(): terms.append(lax.ppermute(sums[s], 'ka', turn))  5.32 us
    ppermute x1, waiting for transfers between devices, on_device(): received = lax.ppermute(to_other, 'vib', swap)  1.9 us
    pallas_call x1, Pallas kernels, on_device(): pl.pallas_call(functools.partial(pack_kernel, chunks), out_shape=[jax.Sha...  1.33 us
  transfers between devices with their start and end apart: 9, of which 4 were waited for; matrix products, arithmetic and copies ran while one was open for 0% of the time, Pallas kernels for 17%

profile of v3, /device:TPU:30, one launch (start us, length us, event | category | flops | bytes accessed | tf_op | source)
XLA Modules:
  0.0 48.8 jit_solution(17571643112317660468)
XLA Ops:
  0.0 0.0 collective-permute-start
  0.0 1.3 %pack.1 = (bf16[1024,256]{1,0:T(8,128)(2,1)S(1)}, bf16[1024,256]{1,0:T(8,128)(2,1)S(1)}) custom-call(s32[2]{0:T(128)} %counts.5, bf16[2,1024,256]{2,1,0:T(8,128)(2,1)} %final.1), custom_call_target="tpu_custom_call" | custom-call | bytes 2097152 | tf_op jit(solution)/shard_map/pack/pallas_call | solution.py:190
  1.3 0.5 %collective-permute-start.1 = (bf16[1024,256]{1,0:T(8,128)(2,1)S(1)}, bf16[1024,256]{1,0:T(8,128)(2,1)S(1)}, u32[]{:S(2)}, u32[]{:S(2)}) collective-permute-start(bf16[1024,256]{1,0:T(8,128)(2,1)S(1)} %get-tuple-element.11.rest_0_), channel_id=1, source_target_pairs={{0,4},{4,0},{8,12},{12,8},{1,5},{5,1},{9,13},{13,9},{2,6},{6,2},{1... | collective-permute-start | bytes 1572872 | tf_op jit(solution)/shard_map/ppermute | solution.py:207
  1.9 0.0 copy-start
  1.9 0.8 %collective-permute-start.3 = (bf16[1024,256]{1,0:T(8,128)(2,1)S(1)}, bf16[1024,256]{1,0:T(8,128)(2,1)S(1)}, u32[]{:S(2)}, u32[]{:S(2)}) collective-permute-start(bf16[1024,256]{1,0:T(8,128)(2,1)S(1)} %get-tuple-element.12.rest_1_), channel_id=1, source_target_pairs={{0,0},{4,8},{8,4},{12,12},{1,1},{5,9},{9,5},{13,13},{2,2},{6,10},{... | collective-permute-start | bytes 1572872 | tf_op jit(solution)/shard_map/ppermute | solution.py:208
  2.7 13.1 %collective-permute-done.1.pair_mine = bf16[1024,256]{1,0:T(8,128)(2,1)S(1)} collective-permute-done((bf16[1024,256]{1,0:T(8,128)(2,1)S(1)}, bf16[1024,256]{1,0:T(8,128)(2,1)S(1)}, u32[]{:S(2)}, u32[]{:S(2)}) %collective-permute-start.1) | collective-permute-done | bytes 524320 | tf_op jit(solution)/shard_map/ppermute | solution.py:207
  15.7 0.0 collective-permute-start.2
  15.7 0.0 collective-permute-done.3.next_mine
  15.7 0.5 %collective-permute-start.4 = (bf16[1024,256]{1,0:T(8,128)(2,1)S(1)}, bf16[1024,256]{1,0:T(8,128)(2,1)S(1)}, u32[]{:S(2)}, u32[]{:S(2)}) collective-permute-start(bf16[1024,256]{1,0:T(8,128)(2,1)S(1)} %collective-permute-done.3.next_mine), channel_id=1, source_target_pairs={{0,2},{2,0},{1,3},{3,1},{4,6},{6,4},{5,7},{7,5},{8,10},{10,8},{9,1... | collective-permute-start | bytes 1572872 | tf_op jit(solution)/shard_map/ppermute | solution.py:235
  16.3 0.0 collective-permute-done.other
  16.3 7.0 %own.1 = (f32[1024,512]{1,0:T(8,128)S(1)}, bf16[1024,2048]{1,0:T(8,128)(2,1)S(1)}) custom-call(s32[2]{0:T(128)} %counts.5, bf16[2,1024,2048]{2,1,0:T(8,128)(2,1)} %moments.1, bf16[2,1024,256]{2,1,0:T(8,128)(2,1)S(1)} %collective-permute-done.other, bf16[1024,256]{1,0:T(8,128)(2,1)S(1)} %get-tuple-element.11.rest_0_, ...), custom_call_target="tpu_custom_call" | custom-call | flops 4294967296 | bytes 10485760 | tf_op jit(solution)/shard_map/own/pallas_call | solution.py:212
  23.2 0.0 collective-permute-done.2.pair_other
  23.2 0.0 collective-permute-done.4.next_other
  23.3 0.0 copy-done
  23.3 5.5 %halo.1 = (f32[512,256]{1,0:T(8,128)S(1)}, f32[512,256]{1,0:T(8,128)S(1)}) custom-call(s32[2]{0:T(128)} %counts.5, bf16[1024,2048]{1,0:T(8,128)(2,1)S(1)} %get-tuple-element.13.cross, bf16[1024,256]{1,0:T(8,128)(2,1)S(1)} %collective-permute-done.1.pair_mine, bf16[1024,256]{1,0:T(8,128)(2,1)S(1)} %collective-permute-done.2.pair_other, ...), custom_call_target="tpu_custom_call" | custom-call | flops 4294967296 | bytes 8388608 | tf_op jit(solution)/shard_map/halo/pallas_call | solution.py:236
  28.8 0.1 collective-permute-start.5
  28.8 1.9 %collective-permute-done.5 = f32[512,256]{1,0:T(8,128)S(1)} collective-permute-done((f32[512,256]{1,0:T(8,128)S(1)}, f32[512,256]{1,0:T(8,128)S(1)}, u32[]{:S(2)}, u32[]{:S(2)}) %collective-permute-start.5) | collective-permute-done | bytes 524320 | tf_op jit(solution)/shard_map/ppermute | solution.py:258
  30.7 0.1 add.12
  30.9 0.3 collective-permute-start.6
  31.1 4.8 %collective-permute-start.7 = (f32[128,256]{1,0:T(8,128)S(1)}, f32[128,256]{1,0:T(8,128)S(1)}, u32[]{:S(2)}, u32[]{:S(2)}) collective-permute-start(f32[128,256]{1,0:T(8,128)S(1)} %get-tuple-element.19), channel_id=1, source_target_pairs={{0,8},{4,12},{8,0},{12,4},{1,9},{5,13},{9,1},{13,5},{2,10},{6,14},... | collective-permute-start | bytes 393224 | tf_op jit(solution)/shard_map/ppermute | solution.py:263
  35.9 0.3 collective-permute-start.8
  36.2 2.3 %collective-permute-done.6 = f32[128,256]{1,0:T(8,128)S(1)} collective-permute-done((f32[128,256]{1,0:T(8,128)S(1)}, f32[128,256]{1,0:T(8,128)S(1)}, u32[]{:S(2)}, u32[]{:S(2)}) %collective-permute-start.6) | collective-permute-done | bytes 131104 | tf_op jit(solution)/shard_map/ppermute | solution.py:263
  38.5 9.6 %collective-permute-done.7 = f32[128,256]{1,0:T(8,128)S(1)} collective-permute-done((f32[128,256]{1,0:T(8,128)S(1)}, f32[128,256]{1,0:T(8,128)S(1)}, u32[]{:S(2)}, u32[]{:S(2)}) %collective-permute-start.7) | collective-permute-done | bytes 131104 | tf_op jit(solution)/shard_map/ppermute | solution.py:263
  48.1 0.0 collective-permute-done.8
  48.1 0.7 %fusion.2 = f32[128,256]{1,0:T(8,128)} fusion(f32[128,256]{1,0:T(8,128)S(1)} %collective-permute-done.8, f32[128,256]{1,0:T(8,128)S(1)} %collective-permute-done.7, f32[128,256]{1,0:T(8,128)S(1)} %collective-permute-done.6, f32[512,256]{1,0:T(8,128)S(1)} %add.12), kind=kLoop, calls=%fused_computation.3 | loop fusion | flops 131072 | bytes 655360 | tf_op jit(solution)/shard_map/mul | solution.py:271
  (1 shorter events, 0.0 us)
Async XLA Ops:
  0.0 16.3 %collective-permute-start = (bf16[2,1024,256]{2,1,0:T(8,128)(2,1)}, bf16[2,1024,256]{2,1,0:T(8,128)(2,1)S(1)}, u32[]{:S(2)}, u32[]{:S(2)}) collective-permute-start(bf16[2,1024,256]{2,1,0:T(8,128)(2,1)} %final.1), channel_id=1, source_target_pairs={{0,2},{2,0},{1,3},{3,1},{4,6},{6,4},{5,7},{7,5},{8,10},{10,8},{9,1... | collective-permute-start | bytes 3145736 | tf_op jit(solution)/shard_map/ppermute | solution.py:210
  1.3 14.4 %collective-permute-start.1 = (bf16[1024,256]{1,0:T(8,128)(2,1)S(1)}, bf16[1024,256]{1,0:T(8,128)(2,1)S(1)}, u32[]{:S(2)}, u32[]{:S(2)}) collective-permute-start(bf16[1024,256]{1,0:T(8,128)(2,1)S(1)} %get-tuple-element.11.rest_0_), channel_id=1, source_target_pairs={{0,4},{4,0},{8,12},{12,8},{1,5},{5,1},{9,13},{13,9},{2,6},{6,2},{1... | collective-permute-start | bytes 1572872 | tf_op jit(solution)/shard_map/ppermute | solution.py:207
  1.9 21.4 %copy-start = (bf16[2,1024,1024]{2,1,0:T(8,128)(2,1)S(1)}, bf16[2,1024,1024]{2,1,0:T(8,128)(2,1)}, u32[]{:S(2)}) copy-start(bf16[2,1024,1024]{2,1,0:T(8,128)(2,1)} %initial.1) | copy-start | bytes 12582916
  1.9 13.9 %collective-permute-start.3 = (bf16[1024,256]{1,0:T(8,128)(2,1)S(1)}, bf16[1024,256]{1,0:T(8,128)(2,1)S(1)}, u32[]{:S(2)}, u32[]{:S(2)}) collective-permute-start(bf16[1024,256]{1,0:T(8,128)(2,1)S(1)} %get-tuple-element.12.rest_1_), channel_id=1, source_target_pairs={{0,0},{4,8},{8,4},{12,12},{1,1},{5,9},{9,5},{13,13},{2,2},{6,10},{... | collective-permute-start | bytes 1572872 | tf_op jit(solution)/shard_map/ppermute | solution.py:208
  15.7 7.5 %collective-permute-start.2 = (bf16[1024,256]{1,0:T(8,128)(2,1)S(1)}, bf16[1024,256]{1,0:T(8,128)(2,1)S(1)}, u32[]{:S(2)}, u32[]{:S(2)}) collective-permute-start(bf16[1024,256]{1,0:T(8,128)(2,1)S(1)} %collective-permute-done.1.pair_mine), channel_id=1, source_target_pairs={{0,2},{2,0},{1,3},{3,1},{4,6},{6,4},{5,7},{7,5},{8,10},{10,8},{9,1... | collective-permute-start | bytes 1572872 | tf_op jit(solution)/shard_map/ppermute | solution.py:234
  15.7 7.5 %collective-permute-start.4 = (bf16[1024,256]{1,0:T(8,128)(2,1)S(1)}, bf16[1024,256]{1,0:T(8,128)(2,1)S(1)}, u32[]{:S(2)}, u32[]{:S(2)}) collective-permute-start(bf16[1024,256]{1,0:T(8,128)(2,1)S(1)} %collective-permute-done.3.next_mine), channel_id=1, source_target_pairs={{0,2},{2,0},{1,3},{3,1},{4,6},{6,4},{5,7},{7,5},{8,10},{10,8},{9,1... | collective-permute-start | bytes 1572872 | tf_op jit(solution)/shard_map/ppermute | solution.py:235
  28.8 2.0 %collective-permute-start.5 = (f32[512,256]{1,0:T(8,128)S(1)}, f32[512,256]{1,0:T(8,128)S(1)}, u32[]{:S(2)}, u32[]{:S(2)}) collective-permute-start(f32[512,256]{1,0:T(8,128)S(1)} %get-tuple-element.16), channel_id=1, source_target_pairs={{0,2},{2,0},{1,3},{3,1},{4,6},{6,4},{5,7},{7,5},{8,10},{10,8},{9,1... | collective-permute-start | bytes 1572872 | tf_op jit(solution)/shard_map/ppermute | solution.py:258
  30.9 7.6 %collective-permute-start.6 = (f32[128,256]{1,0:T(8,128)S(1)}, f32[128,256]{1,0:T(8,128)S(1)}, u32[]{:S(2)}, u32[]{:S(2)}) collective-permute-start(f32[128,256]{1,0:T(8,128)S(1)} %get-tuple-element.17), channel_id=1, source_target_pairs={{0,4},{4,8},{8,12},{12,0},{1,5},{5,9},{9,13},{13,1},{2,6},{6,10},{... | collective-permute-start | bytes 393224 | tf_op jit(solution)/shard_map/ppermute | solution.py:263
  31.1 16.9 %collective-permute-start.7 = (f32[128,256]{1,0:T(8,128)S(1)}, f32[128,256]{1,0:T(8,128)S(1)}, u32[]{:S(2)}, u32[]{:S(2)}) collective-permute-start(f32[128,256]{1,0:T(8,128)S(1)} %get-tuple-element.19), channel_id=1, source_target_pairs={{0,8},{4,12},{8,0},{12,4},{1,9},{5,13},{9,1},{13,5},{2,10},{6,14},... | collective-permute-start | bytes 393224 | tf_op jit(solution)/shard_map/ppermute | solution.py:263
  35.9 12.2 %collective-permute-start.8 = (f32[128,256]{1,0:T(8,128)S(1)}, f32[128,256]{1,0:T(8,128)S(1)}, u32[]{:S(2)}, u32[]{:S(2)}) collective-permute-start(f32[128,256]{1,0:T(8,128)S(1)} %get-tuple-element.18), channel_id=1, source_target_pairs={{0,12},{4,0},{8,4},{12,8},{1,13},{5,1},{9,5},{13,9},{2,14},{6,2},{... | collective-permute-start | bytes 393224 | tf_op jit(solution)/shard_map/ppermute | solution.py:263

commit v4 on v3

v4 whole, which is shorter than its diff:
```python
import functools

import jax
import jax.numpy as jnp
from jax import lax
from jax.experimental import pallas as pl
from jax.experimental.pallas import tpu as pltpu
from jax.sharding import PartitionSpec as P


JQ = 30
BF16, F32 = jnp.bfloat16, jnp.float32
TINY = 1e-30
SCALE_ROWS = 16


def couplings(position, kblocks, width):
    total = lax.axis_size("ka") * kblocks
    jsquare = float(JQ * (JQ + 1))
    norm = jnp.sqrt(jnp.full((1, width), jsquare, F32))

    def k_value(k):
        return jnp.full((1, width), (k - total // 2).astype(F32), F32)

    first = position * kblocks
    rows = []
    for j in range(kblocks):
        k = first + j
        here, under, over = k_value(k), k_value(k - 1), k_value(k + 1)
        upper = 0.5 * jnp.sqrt(jnp.maximum(jsquare - under * (under + 1.0), 0.0)) / norm
        lower = -0.5 * jnp.sqrt(jnp.maximum(jsquare - over * (over - 1.0), 0.0)) / norm
        upper = jnp.where(k > 0, upper, 0.0)
        lower = jnp.where(k < total - 1, lower, 0.0)
        rows.append((here / norm, upper, lower))
    return rows


def keep_rows(x, count, start):
    row = lax.broadcasted_iota(jnp.int32, x.shape, 0) + start
    return jnp.where(row < count, x.astype(F32), 0.0).astype(x.dtype)


def pack_kernel(counts, final, near, far, held, live, sems):
    position, core = lax.axis_index("ka"), lax.axis_index("vib")
    parity = lax.rem(position, 2)
    rows = near.shape[0]
    sizes = pltpu.make_async_copy(counts, live, sems.at[2])
    sizes.start()
    copies = []
    for slot, k in enumerate((1 - parity, parity)):
        copies.append(pltpu.make_async_copy(final.at[k], held.at[slot], sems.at[slot]))
        copies[-1].start()
    sizes.wait()
    for slot, (k, out) in enumerate(((1 - parity, near), (parity, far))):
        copies[slot].wait()
        out[...] = keep_rows(held[slot], live[k], core * rows)


def own_kernel(block, counts, moments, other, near, far, out, rhs, live, sems):
    position, core = lax.axis_index("ka"), lax.axis_index("vib")
    parity = lax.rem(position, 2)
    kblocks, rows, width = other.shape
    sizes = pltpu.make_async_copy(counts, live, sems.at[0])
    sizes.start()
    mine_at = pl.multiple_of(core * rows, rows)
    other_at = pl.multiple_of((1 - core) * rows, rows)
    for k, source in ((1 - parity, near), (parity, far)):
        at = pl.multiple_of(k * width, width)
        rhs[pl.ds(mine_at, rows), pl.ds(at, width)] = source[...]
    sizes.wait()
    for k in range(kblocks):
        rhs[pl.ds(other_at, rows), k * width : (k + 1) * width] = keep_rows(
            other[k], live[k], other_at
        )

    (same_low, _, lower), (same_high, upper, _) = couplings(position, kblocks, width)
    for start in range(0, rows, block):
        v = slice(start, start + block)
        z = jnp.dot(moments[0, v, :], rhs[...], preferred_element_type=F32)
        x = jnp.dot(moments[1, v, :], rhs[...], preferred_element_type=F32)
        out[v, :width] = same_low * z[:, :width] + lower * x[:, width:]
        out[v, width:] = same_high * z[:, width:] + upper * x[:, :width]


def side_kernel(places, block, is_near, counts, moments, mine, other, partial, initial, *rest):
    if is_near:
        total, images, live, sems = rest
    else:
        before, to_other, to_own, images, total, live, sems = rest
    sizes = pltpu.make_async_copy(counts, live, sems.at[0])
    sizes.start()
    position, core = lax.axis_index("ka"), lax.axis_index("vib")
    parity = lax.rem(position, 2)
    k = 1 - parity if is_near else parity
    rows, width = mine.shape
    states = initial.shape[2]
    mine_at = pl.multiple_of(core * rows, rows)
    other_at = pl.multiple_of((1 - core) * rows, rows)
    columns = pl.ds(pl.multiple_of(k * width, width), width)
    (_, upper, _), (_, _, lower) = couplings(position, 2, width)
    weight = jnp.where(k == 0, upper, lower)
    sizes.wait()

    for v in range(0, rows, block):
        at = slice(v, v + block)
        x = jnp.dot(
            moments[1, at, pl.ds(mine_at, rows)], mine[...], preferred_element_type=F32
        ) + jnp.dot(
            moments[1, at, pl.ds(other_at, rows)], other[...], preferred_element_type=F32
        )
        row = lax.broadcasted_iota(jnp.int32, (block, width), 0) + core * rows + v
        image = partial[at, columns] + weight * x
        image = jnp.where(row < live[k], image, 0.0)
        high = image.astype(BF16)
        images[at, :width] = high
        images[at, width:] = (image - high.astype(F32)).astype(BF16)

    for i in range(0, states, block):
        both = lax.dot_general(
            initial[k, :, i : i + block],
            images[...],
            (((0,), (0,)), ((), ())),
            preferred_element_type=F32,
        )
        both = both[:, :width] + both[:, width:]
        total[i : i + block, :] = both if is_near else both + before[i : i + block, :]

    if is_near:
        return
    share = to_own.shape[0] // places
    for s in range(places):
        dest = lax.rem(position + s, places)
        own_at = pl.multiple_of((dest * 2 + core) * share, share)
        other_at = pl.multiple_of((dest * 2 + 1 - core) * share, share)
        to_own[s * share : (s + 1) * share, :] = total[pl.ds(own_at, share), :]
        to_other[s * share : (s + 1) * share, :] = total[pl.ds(other_at, share), :]


def code_kernel(mine, other, own, *outs):
    share, width = own.shape
    own[...] = mine[:share, :] + other[:share, :]
    for s, out in enumerate(outs, 1):
        rows = slice(s * share, (s + 1) * share)
        value = mine[rows, :] + other[rows, :]
        peak = jnp.maximum(jnp.max(jnp.abs(value), axis=0, keepdims=True), TINY)
        exponent = jnp.floor(jnp.log2(peak)) + 1.0
        code = jnp.floor(value * jnp.exp2(15.0 - exponent) + 0.5)
        code = jnp.clip(code, -32767.0, 32767.0)
        out[:share, :] = code.astype(jnp.int32).astype(jnp.int16)
        spread = jnp.broadcast_to(exponent, (out.shape[0] - share, width))
        out[share:, :] = spread.astype(jnp.int32).astype(jnp.int16)


def decode(coded, share):
    exponent = coded[share : share + 1].astype(F32)
    return coded[:share].astype(F32) * jnp.exp2(exponent - 15.0)


def cost(flops, moved):
    return pl.CostEstimate(flops=int(flops), bytes_accessed=int(moved), transcendentals=0)


def kernel_params(mib):
    return pltpu.CompilerParams(vmem_limit_bytes=mib << 20)


def on_device(moments, initial_vectors, final_vectors, basis_counts):
    kblocks, rows, states = initial_vectors.shape
    width = final_vectors.shape[2]
    whole = moments.shape[2]
    places, cores = lax.axis_size("ka"), lax.axis_size("vib")
    if kblocks != 2 or cores != 2 or places % 2:
        raise ValueError("unsupported mesh")
    share = states // (places * cores)
    half = states // cores
    block = 256

    def resting(x):
        return pltpu.with_memory_space_constraint(x, pltpu.HBM)

    swap = [(0, 1), (1, 0)]
    pair = [(a, a + 1 - 2 * (a % 2)) for a in range(places)]
    other_side = [(a, min(max(a - 1 + 2 * (a % 2), 0), places - 1)) for a in range(places)]
    vmem = pl.BlockSpec(memory_space=pltpu.VMEM)
    hbm = pl.BlockSpec(memory_space=pltpu.HBM)
    counted = pltpu.SMEM((kblocks,), jnp.int32)
    counts = resting(basis_counts)

    near_out, far_out = pl.pallas_call(
        pack_kernel,
        out_shape=[jax.ShapeDtypeStruct((rows, width), BF16)] * 2,
        in_specs=[hbm, hbm],
        out_specs=[vmem] * 2,
        scratch_shapes=[
            pltpu.VMEM((kblocks, rows, width), BF16),
            counted,
            pltpu.SemaphoreType.DMA((3,)),
        ],
        cost_estimate=cost(8 * rows * whole * width, 4 * kblocks * rows * width),
        compiler_params=kernel_params(8),
        name="pack",
    )(counts, resting(final_vectors))

    near = lax.ppermute(near_out, "ka", pair)
    far = lax.ppermute(far_out, "ka", other_side)
    final_other = lax.ppermute(final_vectors, "vib", swap)

    partial = pl.pallas_call(
        functools.partial(own_kernel, block),
        out_shape=jax.ShapeDtypeStruct((rows, kblocks * width), F32),
        in_specs=[hbm] + [vmem] * 4,
        out_specs=vmem,
        scratch_shapes=[
            pltpu.VMEM((whole, kblocks * width), BF16),
            counted,
            pltpu.SemaphoreType.DMA((1,)),
        ],
        cost_estimate=cost(4 * rows * whole * kblocks * width, 8 * rows * width),
        compiler_params=kernel_params(20),
        name="own",
    )(counts, moments, final_other, near_out, far_out)

    def side(is_near, mine, other, *before):
        outs = [jax.ShapeDtypeStruct((states, width), F32)]
        scratch = [
            pltpu.VMEM((rows, 2 * width), BF16),
            counted,
            pltpu.SemaphoreType.DMA((1,)),
        ]
        if not is_near:
            outs = [jax.ShapeDtypeStruct((half, width), F32)] * 2
            scratch.insert(1, pltpu.VMEM((states, width), F32))
        return pl.pallas_call(
            functools.partial(side_kernel, places, block, is_near),
            out_shape=outs,
            in_specs=[hbm] + [vmem] * (5 + len(before)),
            out_specs=[vmem] * len(outs),
            scratch_shapes=scratch,
            cost_estimate=cost(
                2 * rows * whole * width + 4 * rows * states * width, 4 * rows * states
            ),
            compiler_params=kernel_params(20),
            name="side",
        )(counts, moments, mine, other, partial, initial_vectors, *before)

    near_other = lax.ppermute(near, "vib", swap)
    (before,) = side(True, near, near_other)
    far_other = lax.ppermute(far, "vib", swap)
    to_other, to_own = side(False, far, far_other, before)

    received = lax.ppermute(to_other, "vib", swap)
    amplitude, *coded = pl.pallas_call(
        code_kernel,
        out_shape=[jax.ShapeDtypeStruct((share, width), F32)]
        + [jax.ShapeDtypeStruct((share + SCALE_ROWS, width), jnp.int16)] * (places - 1),
        in_specs=[vmem] * 2,
        out_specs=[vmem] * places,
        cost_estimate=cost(16 * half * width, 12 * half * width),
        compiler_params=kernel_params(8),
        name="code",
    )(to_own, received)
    for s in range(1, places):
        turn = [(a, (a + s) % places) for a in range(places)]
        arrived = lax.ppermute(coded[s - 1], "ka", turn)
        amplitude = amplitude + decode(arrived, share)
    return amplitude * amplitude


def solution(mesh):
    in_specs = (
        P(None, "vib", None),
        P("ka", "vib", "grp"),
        P("ka", "vib", ("grp", "fin")),
        P(("grp", "ka")),
    )
    out_specs = P(("grp", "ka", "vib"), "fin")

    return jax.shard_map(
        on_device, mesh=mesh, in_specs=in_specs, out_specs=out_specs, check_vma=False
    )
```

time: 48.9 us -> 45.2 us (0.924)
  the two profiles are of different devices: /device:TPU:30 before, /device:TPU:0 now
where the time goes in v4:
time: 45.2 us; the launch traced here: 45 us
  waiting for transfers between devices  17.2 us (38%)
  Pallas kernels  13.7 us (30%)
  starting transfers between devices  13.3 us (29%)
  other arithmetic  0.78 us (2%)
    ppermute x1, waiting for transfers between devices, on_device(): near = lax.ppermute(near_out, 'ka', pair)  11.9 us
    ppermute x3, starting transfers between devices, on_device(): arrived = lax.ppermute(coded[s - 1], 'ka', turn)  8.81 us
    pallas_call x2, Pallas kernels, side(): pl.pallas_call(functools.partial(side_kernel, places, block, is_near), ou...  6.49 us
    pallas_call x1, Pallas kernels, on_device(): pl.pallas_call(functools.partial(own_kernel, block), out_shape=jax.ShapeD...  5.47 us
    ppermute x3, waiting for transfers between devices, on_device(): arrived = lax.ppermute(coded[s - 1], 'ka', turn)  3.43 us
    ppermute x1, starting transfers between devices, on_device(): near = lax.ppermute(near_out, 'ka', pair)  2.59 us
    ppermute x1, waiting for transfers between devices, on_device(): received = lax.ppermute(to_other, 'vib', swap)  1.85 us
    pallas_call x1, Pallas kernels, on_device(): pl.pallas_call(pack_kernel, out_shape=[jax.ShapeDtypeStruct((rows, width)...  1.53 us
  transfers between devices with their start and end apart: 9, of which 3 were waited for; matrix products, arithmetic and copies ran while one was open for 0% of the time, Pallas kernels for 23%

profile of v4, /device:TPU:0, one launch (start us, length us, event | category | flops | bytes accessed | tf_op | source)
XLA Modules:
  0.0 45.0 jit_solution(2750661559685083287)
XLA Ops:
  0.0 0.0 copy-start
  0.0 0.5 %collective-permute-start.2 = (bf16[2,1024,256]{2,1,0:T(8,128)(2,1)}, bf16[2,1024,256]{2,1,0:T(8,128)(2,1)S(1)}, u32[]{:S(2)}, u32[]{:S(2)}) collective-permute-start(bf16[2,1024,256]{2,1,0:T(8,128)(2,1)} %final.1), channel_id=1, source_target_pairs={{0,2},{2,0},{1,3},{3,1},{4,6},{6,4},{5,7},{7,5},{8,10},{10,8},{9,1... | collective-permute-start | bytes 3145736 | tf_op jit(solution)/shard_map/ppermute | solution.py:206
  0.5 1.5 %pack.1 = (bf16[1024,256]{1,0:T(8,128)(2,1)S(1)}, bf16[1024,256]{1,0:T(8,128)(2,1)S(1)}) custom-call(s32[2]{0:T(128)} %counts.7, bf16[2,1024,256]{2,1,0:T(8,128)(2,1)} %final.1), custom_call_target="tpu_custom_call" | custom-call | flops 4294967296 | bytes 2097152 | tf_op jit(solution)/shard_map/pack/pallas_call | solution.py:189
  2.0 2.6 %collective-permute-start.3 = (bf16[1024,256]{1,0:T(8,128)(2,1)S(1)}, bf16[1024,256]{1,0:T(8,128)(2,1)S(1)}, u32[]{:S(2)}, u32[]{:S(2)}) collective-permute-start(bf16[1024,256]{1,0:T(8,128)(2,1)S(1)} %get-tuple-element.14.near), channel_id=1, source_target_pairs={{0,4},{4,0},{8,12},{12,8},{1,5},{5,1},{9,13},{13,9},{2,6},{6,2},{1... | collective-permute-start | bytes 1572872 | tf_op jit(solution)/shard_map/ppermute | solution.py:204
  4.6 0.0 copy-start.1
  4.6 0.8 %collective-permute-start = (bf16[1024,256]{1,0:T(8,128)(2,1)S(1)}, bf16[1024,256]{1,0:T(8,128)(2,1)S(1)}, u32[]{:S(2)}, u32[]{:S(2)}) collective-permute-start(bf16[1024,256]{1,0:T(8,128)(2,1)S(1)} %get-tuple-element.13.far), channel_id=1, source_target_pairs={{0,0},{4,8},{8,4},{12,12},{1,1},{5,9},{9,5},{13,13},{2,2},{6,10},{... | collective-permute-start | bytes 1572872 | tf_op jit(solution)/shard_map/ppermute | solution.py:205
  5.4 11.9 %collective-permute-done.3.mine = bf16[1024,256]{1,0:T(8,128)(2,1)S(1)} collective-permute-done((bf16[1024,256]{1,0:T(8,128)(2,1)S(1)}, bf16[1024,256]{1,0:T(8,128)(2,1)S(1)}, u32[]{:S(2)}, u32[]{:S(2)}) %collective-permute-start.3) | collective-permute-done | bytes 524320 | tf_op jit(solution)/shard_map/ppermute | solution.py:204
  17.3 0.0 collective-permute-start.4
  17.4 0.0 collective-permute-done.mine
  17.4 0.5 %collective-permute-start.1 = (bf16[1024,256]{1,0:T(8,128)(2,1)S(1)}, bf16[1024,256]{1,0:T(8,128)(2,1)S(1)}, u32[]{:S(2)}, u32[]{:S(2)}) collective-permute-start(bf16[1024,256]{1,0:T(8,128)(2,1)S(1)} %collective-permute-done.mine), channel_id=1, source_target_pairs={{0,2},{2,0},{1,3},{3,1},{4,6},{6,4},{5,7},{7,5},{8,10},{10,8},{9,1... | collective-permute-start | bytes 1572872 | tf_op jit(solution)/shard_map/ppermute | solution.py:248
  17.9 0.0 collective-permute-done.2.other
  17.9 0.0 copy-done
  17.9 5.5 %own.1.partial = f32[1024,512]{1,0:T(8,128)S(1)} custom-call(s32[2]{0:T(128)} %counts.7, bf16[2,1024,2048]{2,1,0:T(8,128)(2,1)S(1)} %copy-done, bf16[2,1024,256]{2,1,0:T(8,128)(2,1)S(1)} %collective-permute-done.2.other, bf16[1024,256]{1,0:T(8,128)(2,1)S(1)} %get-tuple-element.14.near, bf16[1024,256]{1,0:T(8,128)(2,1)S(1)} %get-tuple-element.13.far), custom_call_target="tpu_custom_call" | custom-call | flops 4294967296 | bytes 2097152 | tf_op jit(solution)/shard_map/own/pallas_call | solution.py:208
  23.3 0.0 collective-permute-done.4.other
  23.3 0.0 copy-done.1
  23.4 3.2 %side.2.rest_0_ = f32[1024,256]{1,0:T(8,128)S(1)} custom-call(s32[2]{0:T(128)} %counts.7, bf16[2,1024,2048]{2,1,0:T(8,128)(2,1)S(1)} %copy-done, bf16[1024,256]{1,0:T(8,128)(2,1)S(1)} %collective-permute-done.3.mine, bf16[1024,256]{1,0:T(8,128)(2,1)S(1)} %collective-permute-done.4.other, f32[1024,512]{1,0:T(8,128)S(1)} %own.1.partial, ...), custom_call_target="tpu_custom_call" | custom-call | flops 2147483648 | bytes 4194304 | tf_op jit(solution)/shard_map/side/pallas_call | solution.py:233
  26.6 0.0 collective-permute-done.1.other
  26.6 3.3 %side.3 = (f32[512,256]{1,0:T(8,128)S(1)}, f32[512,256]{1,0:T(8,128)S(1)}) custom-call(s32[2]{0:T(128)} %counts.7, bf16[2,1024,2048]{2,1,0:T(8,128)(2,1)S(1)} %copy-done, bf16[1024,256]{1,0:T(8,128)(2,1)S(1)} %collective-permute-done.mine, bf16[1024,256]{1,0:T(8,128)(2,1)S(1)} %collective-permute-done.1.other, f32[1024,512]{1,0:T(8,128)S(1)} %own.1.partial, ...), custom_call_target="tpu_custom_call" | custom-call | flops 2147483648 | bytes 4194304 | tf_op jit(solution)/shard_map/side/pallas_call | solution.py:233
  29.9 0.1 collective-permute-start.5
  30.0 1.9 %collective-permute-done.5.other = f32[512,256]{1,0:T(8,128)S(1)} collective-permute-done((f32[512,256]{1,0:T(8,128)S(1)}, f32[512,256]{1,0:T(8,128)S(1)}, u32[]{:S(2)}, u32[]{:S(2)}) %collective-permute-start.5) | collective-permute-done | bytes 524320 | tf_op jit(solution)/shard_map/ppermute | solution.py:251
  31.8 0.2 code.1
  32.0 4.7 %collective-permute-start.6 = (s16[144,256]{1,0:T(8,128)(2,1)S(1)}, s16[144,256]{1,0:T(8,128)(2,1)S(1)}, u32[]{:S(2)}, u32[]{:S(2)}) collective-permute-start(s16[144,256]{1,0:T(8,128)(2,1)S(1)} %get-tuple-element.18), channel_id=1, source_target_pairs={{0,4},{4,8},{8,12},{12,0},{1,5},{5,9},{9,13},{13,1},{2,6},{6,10},{... | collective-permute-start | bytes 221192 | tf_op jit(solution)/shard_map/ppermute | solution.py:264
  36.7 1.3 %collective-permute-start.7 = (s16[144,256]{1,0:T(8,128)(2,1)S(1)}, s16[144,256]{1,0:T(8,128)(2,1)S(1)}, u32[]{:S(2)}, u32[]{:S(2)}) collective-permute-start(s16[144,256]{1,0:T(8,128)(2,1)S(1)} %get-tuple-element.19), channel_id=1, source_target_pairs={{0,8},{4,12},{8,0},{12,4},{1,9},{5,13},{9,1},{13,5},{2,10},{6,14},... | collective-permute-start | bytes 221192 | tf_op jit(solution)/shard_map/ppermute | solution.py:264
  38.0 2.8 %collective-permute-start.8 = (s16[144,256]{1,0:T(8,128)(2,1)S(1)}, s16[144,256]{1,0:T(8,128)(2,1)S(1)}, u32[]{:S(2)}, u32[]{:S(2)}) collective-permute-start(s16[144,256]{1,0:T(8,128)(2,1)S(1)} %get-tuple-element.20), channel_id=1, source_target_pairs={{0,12},{4,0},{8,4},{12,8},{1,13},{5,1},{9,5},{13,9},{2,14},{6,2},{... | collective-permute-start | bytes 221192 | tf_op jit(solution)/shard_map/ppermute | solution.py:264
  40.8 0.0 collective-permute-done.6
  40.8 3.4 %collective-permute-done.7 = s16[144,256]{1,0:T(8,128)(2,1)S(1)} collective-permute-done((s16[144,256]{1,0:T(8,128)(2,1)S(1)}, s16[144,256]{1,0:T(8,128)(2,1)S(1)}, u32[]{:S(2)}, u32[]{:S(2)}) %collective-permute-start.7) | collective-permute-done | bytes 73760 | tf_op jit(solution)/shard_map/ppermute | solution.py:264
  44.3 0.0 collective-permute-done.8
  44.3 0.7 %add_multiply_fusion = f32[128,256]{1,0:T(8,128)} fusion(f32[128,256]{1,0:T(8,128)S(1)} %get-tuple-element.17, s16[144,256]{1,0:T(8,128)(2,1)S(1)} %collective-permute-done.8, s16[144,256]{1,0:T(8,128)(2,1)S(1)} %collective-permute-done.7, s16[144,256]{1,0:T(8,128)(2,1)S(1)} %collective-permute-done.6, f32[256]{0:T(256)S(1)} %bitcast.5, f32[256]{0:T(256)S(1)} %bitcast.4, ...), kind=kLoop, calls=%fused_computation | loop fusion | flops 327680 | bytes 461824 | tf_op jit(solution)/shard_map/mul | solution.py:266
  (3 shorter events, 0.0 us)
Async XLA Ops:
  0.0 17.9 %copy-start = (bf16[2,1024,2048]{2,1,0:T(8,128)(2,1)S(1)}, bf16[2,1024,2048]{2,1,0:T(8,128)(2,1)}, u32[]{:S(2)}) copy-start(bf16[2,1024,2048]{2,1,0:T(8,128)(2,1)} %moments.5) | copy-start | bytes 25165828
  0.0 17.9 %collective-permute-start.2 = (bf16[2,1024,256]{2,1,0:T(8,128)(2,1)}, bf16[2,1024,256]{2,1,0:T(8,128)(2,1)S(1)}, u32[]{:S(2)}, u32[]{:S(2)}) collective-permute-start(bf16[2,1024,256]{2,1,0:T(8,128)(2,1)} %final.1), channel_id=1, source_target_pairs={{0,2},{2,0},{1,3},{3,1},{4,6},{6,4},{5,7},{7,5},{8,10},{10,8},{9,1... | collective-permute-start | bytes 3145736 | tf_op jit(solution)/shard_map/ppermute | solution.py:206
  2.0 15.3 %collective-permute-start.3 = (bf16[1024,256]{1,0:T(8,128)(2,1)S(1)}, bf16[1024,256]{1,0:T(8,128)(2,1)S(1)}, u32[]{:S(2)}, u32[]{:S(2)}) collective-permute-start(bf16[1024,256]{1,0:T(8,128)(2,1)S(1)} %get-tuple-element.14.near), channel_id=1, source_target_pairs={{0,4},{4,0},{8,12},{12,8},{1,5},{5,1},{9,13},{13,9},{2,6},{6,2},{1... | collective-permute-start | bytes 1572872 | tf_op jit(solution)/shard_map/ppermute | solution.py:204
  4.6 18.7 %copy-start.1 = (bf16[2,1024,1024]{2,1,0:T(8,128)(2,1)S(1)}, bf16[2,1024,1024]{2,1,0:T(8,128)(2,1)}, u32[]{:S(2)}) copy-start(bf16[2,1024,1024]{2,1,0:T(8,128)(2,1)} %initial.3) | copy-start | bytes 12582916
  4.6 12.8 %collective-permute-start = (bf16[1024,256]{1,0:T(8,128)(2,1)S(1)}, bf16[1024,256]{1,0:T(8,128)(2,1)S(1)}, u32[]{:S(2)}, u32[]{:S(2)}) collective-permute-start(bf16[1024,256]{1,0:T(8,128)(2,1)S(1)} %get-tuple-element.13.far), channel_id=1, source_target_pairs={{0,0},{4,8},{8,4},{12,12},{1,1},{5,9},{9,5},{13,13},{2,2},{6,10},{... | collective-permute-start | bytes 1572872 | tf_op jit(solution)/shard_map/ppermute | solution.py:205
  17.3 6.0 %collective-permute-start.4 = (bf16[1024,256]{1,0:T(8,128)(2,1)S(1)}, bf16[1024,256]{1,0:T(8,128)(2,1)S(1)}, u32[]{:S(2)}, u32[]{:S(2)}) collective-permute-start(bf16[1024,256]{1,0:T(8,128)(2,1)S(1)} %collective-permute-done.3.mine), channel_id=1, source_target_pairs={{0,2},{2,0},{1,3},{3,1},{4,6},{6,4},{5,7},{7,5},{8,10},{10,8},{9,1... | collective-permute-start | bytes 1572872 | tf_op jit(solution)/shard_map/ppermute | solution.py:246
  17.4 9.2 %collective-permute-start.1 = (bf16[1024,256]{1,0:T(8,128)(2,1)S(1)}, bf16[1024,256]{1,0:T(8,128)(2,1)S(1)}, u32[]{:S(2)}, u32[]{:S(2)}) collective-permute-start(bf16[1024,256]{1,0:T(8,128)(2,1)S(1)} %collective-permute-done.mine), channel_id=1, source_target_pairs={{0,2},{2,0},{1,3},{3,1},{4,6},{6,4},{5,7},{7,5},{8,10},{10,8},{9,1... | collective-permute-start | bytes 1572872 | tf_op jit(solution)/shard_map/ppermute | solution.py:248
  29.9 2.0 %collective-permute-start.5 = (f32[512,256]{1,0:T(8,128)S(1)}, f32[512,256]{1,0:T(8,128)S(1)}, u32[]{:S(2)}, u32[]{:S(2)}) collective-permute-start(f32[512,256]{1,0:T(8,128)S(1)} %get-tuple-element.16), channel_id=1, source_target_pairs={{0,2},{2,0},{1,3},{3,1},{4,6},{6,4},{5,7},{7,5},{8,10},{10,8},{9,1... | collective-permute-start | bytes 1572872 | tf_op jit(solution)/shard_map/ppermute | solution.py:251
  32.0 8.8 %collective-permute-start.6 = (s16[144,256]{1,0:T(8,128)(2,1)S(1)}, s16[144,256]{1,0:T(8,128)(2,1)S(1)}, u32[]{:S(2)}, u32[]{:S(2)}) collective-permute-start(s16[144,256]{1,0:T(8,128)(2,1)S(1)} %get-tuple-element.18), channel_id=1, source_target_pairs={{0,4},{4,8},{8,12},{12,0},{1,5},{5,9},{9,13},{13,1},{2,6},{6,10},{... | collective-permute-start | bytes 221192 | tf_op jit(solution)/shard_map/ppermute | solution.py:264
  36.7 7.5 %collective-permute-start.7 = (s16[144,256]{1,0:T(8,128)(2,1)S(1)}, s16[144,256]{1,0:T(8,128)(2,1)S(1)}, u32[]{:S(2)}, u32[]{:S(2)}) collective-permute-start(s16[144,256]{1,0:T(8,128)(2,1)S(1)} %get-tuple-element.19), channel_id=1, source_target_pairs={{0,8},{4,12},{8,0},{12,4},{1,9},{5,13},{9,1},{13,5},{2,10},{6,14},... | collective-permute-start | bytes 221192 | tf_op jit(solution)/shard_map/ppermute | solution.py:264
  38.0 6.3 %collective-permute-start.8 = (s16[144,256]{1,0:T(8,128)(2,1)S(1)}, s16[144,256]{1,0:T(8,128)(2,1)S(1)}, u32[]{:S(2)}, u32[]{:S(2)}) collective-permute-start(s16[144,256]{1,0:T(8,128)(2,1)S(1)} %get-tuple-element.20), channel_id=1, source_target_pairs={{0,12},{4,0},{8,4},{12,8},{1,13},{5,1},{9,5},{13,9},{2,14},{6,2},{... | collective-permute-start | bytes 221192 | tf_op jit(solution)/shard_map/ppermute | solution.py:264

commit v5 on v4

v5 whole, which is shorter than its diff:
```python
import functools

import jax
import jax.numpy as jnp
from jax import lax
from jax.experimental import pallas as pl
from jax.experimental.pallas import tpu as pltpu
from jax.sharding import PartitionSpec as P


JQ = 30
BF16, F32 = jnp.bfloat16, jnp.float32
TINY = 1e-30
SCALE_ROWS = 8


def couplings(position, kblocks, width):
    total = lax.axis_size("ka") * kblocks
    jsquare = float(JQ * (JQ + 1))
    norm = jnp.sqrt(jnp.full((1, width), jsquare, F32))

    def k_value(k):
        return jnp.full((1, width), (k - total // 2).astype(F32), F32)

    first = position * kblocks
    rows = []
    for j in range(kblocks):
        k = first + j
        here, under, over = k_value(k), k_value(k - 1), k_value(k + 1)
        upper = 0.5 * jnp.sqrt(jnp.maximum(jsquare - under * (under + 1.0), 0.0)) / norm
        lower = -0.5 * jnp.sqrt(jnp.maximum(jsquare - over * (over - 1.0), 0.0)) / norm
        upper = jnp.where(k > 0, upper, 0.0)
        lower = jnp.where(k < total - 1, lower, 0.0)
        rows.append((here / norm, upper, lower))
    return rows


def keep_rows(x, count, start):
    row = lax.broadcasted_iota(jnp.int32, x.shape, 0) + start
    return jnp.where(row < count, x.astype(F32), 0.0).astype(x.dtype)


def row_limit(limits, k, width):
    return jnp.concatenate([limits[k, :1, :]] * (width // limits.shape[2]), axis=1)


def side_block(is_near):
    parity = lax.rem(lax.axis_index("ka"), 2)
    return 1 - parity if is_near else parity


def pack_kernel(counts, final, near, far, limits, held, live, sems):
    sizes = pltpu.make_async_copy(counts, live, sems.at[2])
    sizes.start()
    sides = ((side_block(False), far), (side_block(True), near))
    copies = []
    for slot, (k, _) in enumerate(sides):
        copies.append(pltpu.make_async_copy(final.at[k], held.at[slot], sems.at[slot]))
        copies[-1].start()
    sizes.wait()
    for k in range(limits.shape[0]):
        limits[k] = jnp.full(limits.shape[1:], live[k], jnp.int32)
    for slot, (k, out) in enumerate(sides):
        copies[slot].wait()
        out[...] = keep_rows(held[slot], live[k], lax.axis_index("vib") * out.shape[0])


def own_kernel(block, limits, moments, other, near, far, out, rhs):
    position, core = lax.axis_index("ka"), lax.axis_index("vib")
    parity = lax.rem(position, 2)
    kblocks, rows, width = other.shape
    mine_at = pl.multiple_of(core * rows, rows)
    other_at = pl.multiple_of((1 - core) * rows, rows)
    for k, source in ((1 - parity, near), (parity, far)):
        at = pl.multiple_of(k * width, width)
        rhs[pl.ds(mine_at, rows), pl.ds(at, width)] = source[...]
    for k in range(kblocks):
        rhs[pl.ds(other_at, rows), k * width : (k + 1) * width] = keep_rows(
            other[k], row_limit(limits, k, width), other_at
        )

    (same_low, _, lower), (same_high, upper, _) = couplings(position, kblocks, width)
    for start in range(0, rows, block):
        v = slice(start, start + block)
        z = jnp.dot(moments[0, v, :], rhs[...], preferred_element_type=F32)
        x = jnp.dot(moments[1, v, :], rhs[...], preferred_element_type=F32)
        out[v, :width] = same_low * z[:, :width] + lower * x[:, width:]
        out[v, width:] = same_high * z[:, width:] + upper * x[:, :width]


def image_kernel(block, is_near, is_mine, limits, moments, piece, base, out):
    position, core = lax.axis_index("ka"), lax.axis_index("vib")
    k = side_block(is_near)
    rows, width = piece.shape
    half_at = pl.multiple_of((core if is_mine else 1 - core) * rows, rows)
    (_, upper, _), (_, _, lower) = couplings(position, 2, width)
    weight = jnp.where(k == 0, upper, lower)
    columns = pl.ds(pl.multiple_of(k * width, width), width) if is_mine else slice(None)
    limit = row_limit(limits, k, width)
    for v in range(0, rows, block):
        at = slice(v, v + block)
        x = jnp.dot(moments[1, at, pl.ds(half_at, rows)], piece[...], preferred_element_type=F32)
        image = base[at, columns] + weight * x
        if is_mine:
            out[at, :] = image
            continue
        row = lax.broadcasted_iota(jnp.int32, (block, width), 0) + core * rows + v
        image = jnp.where(row < limit, image, 0.0)
        high = image.astype(BF16)
        out[at, :width] = high
        out[at, width:] = (image - high.astype(F32)).astype(BF16)


def product_kernel(places, block, is_near, halves, initial, images, *rest):
    outs, before = rest[-len(halves) :], rest[: -len(halves)]
    position, core = lax.axis_index("ka"), lax.axis_index("vib")
    k = side_block(is_near)
    width = images.shape[1] // 2
    share = outs[0].shape[0] // places
    per = max(1, block // share)
    for h, half in enumerate(halves):
        to_core = core if half == "own" else 1 - core
        offsets = [
            pl.multiple_of((lax.rem(position + s, places) * 2 + to_core) * share, share)
            for s in range(places)
        ]
        for s in range(0, places, per):
            vectors = [initial[k, :, pl.ds(o, share)] for o in offsets[s : s + per]]
            both = lax.dot_general(
                jnp.concatenate(vectors, axis=1),
                images[...],
                (((0,), (0,)), ((), ())),
                preferred_element_type=F32,
            )
            both = both[:, :width] + both[:, width:]
            at = slice(s * share, (s + len(vectors)) * share)
            outs[h][at, :] = both + before[h][at, :] if before else both


def narrow_product_kernel(places, block, is_near, initial, images, *rest):
    to_other, to_own, total = rest[-3:]
    before = rest[:-3]
    position, core = lax.axis_index("ka"), lax.axis_index("vib")
    k = side_block(is_near)
    width = images.shape[1] // 2
    share = to_own.shape[0] // places
    for i in range(0, initial.shape[2], block):
        both = lax.dot_general(
            initial[k, :, i : i + block],
            images[...],
            (((0,), (0,)), ((), ())),
            preferred_element_type=F32,
        )
        total[i : i + block, :] = both[:, :width] + both[:, width:]
    for h, (out, to_core) in enumerate(((to_other, 1 - core), (to_own, core))):
        for s in range(places):
            at = slice(s * share, (s + 1) * share)
            start = (lax.rem(position + s, places) * 2 + to_core) * share
            value = total[pl.ds(pl.multiple_of(start, share), share), :]
            out[at, :] = value + before[h][at, :] if before else value


def code_kernel(mine, other, own, *outs):
    share, width = own.shape
    own[...] = mine[:share, :] + other[:share, :]
    for s, out in enumerate(outs, 1):
        rows = slice(s * share, (s + 1) * share)
        value = mine[rows, :] + other[rows, :]
        peak = jnp.maximum(jnp.max(jnp.abs(value), axis=0, keepdims=True), TINY)
        exponent = jnp.floor(jnp.log2(peak)) + 1.0
        code = jnp.floor(value * jnp.exp2(15.0 - exponent) + 0.5)
        code = jnp.clip(code, -32767.0, 32767.0)
        out[:share, :] = code.astype(jnp.int32).astype(jnp.int16)
        spread = jnp.broadcast_to(exponent, (out.shape[0] - share, width))
        out[share:, :] = spread.astype(jnp.int32).astype(jnp.int16)


def decode(coded, share):
    exponent = coded[share : share + 1].astype(F32)
    return coded[:share].astype(F32) * jnp.exp2(exponent - 15.0)


def cost(flops, moved):
    return pl.CostEstimate(flops=int(flops), bytes_accessed=int(moved), transcendentals=0)


def kernel_params(mib):
    return pltpu.CompilerParams(vmem_limit_bytes=mib << 20)


def on_device(moments, initial_vectors, final_vectors, basis_counts):
    kblocks, rows, states = initial_vectors.shape
    width = final_vectors.shape[2]
    whole = moments.shape[2]
    places, cores = lax.axis_size("ka"), lax.axis_size("vib")
    if kblocks != 2 or cores != 2 or places % 2:
        raise ValueError("unsupported mesh")
    share = states // (places * cores)
    half = states // cores
    block = 256

    def resting(x):
        return pltpu.with_memory_space_constraint(x, pltpu.HBM)

    swap = [(0, 1), (1, 0)]
    pair = [(a, a + 1 - 2 * (a % 2)) for a in range(places)]
    fins = lax.axis_size("fin")
    other_side = []
    for a in range(places):
        to = a - 1 + 2 * (a % 2)
        for x in range(fins):
            inside = 0 <= to < places
            other_side.append((a * fins + x, to * fins + x if inside else a * fins + (x ^ 1) % fins))
    vmem = pl.BlockSpec(memory_space=pltpu.VMEM)
    hbm = pl.BlockSpec(memory_space=pltpu.HBM)

    near_out, far_out, limits = pl.pallas_call(
        pack_kernel,
        out_shape=[jax.ShapeDtypeStruct((rows, width), BF16)] * 2
        + [jax.ShapeDtypeStruct((kblocks, 8, 128), jnp.int32)],
        in_specs=[hbm, hbm],
        out_specs=[vmem] * 3,
        scratch_shapes=[
            pltpu.VMEM((kblocks, rows, width), BF16),
            pltpu.SMEM((kblocks,), jnp.int32),
            pltpu.SemaphoreType.DMA((3,)),
        ],
        cost_estimate=cost(8 * rows * whole * width, 4 * kblocks * rows * width),
        compiler_params=kernel_params(8),
        name="pack",
    )(resting(basis_counts), resting(final_vectors))

    far = lax.ppermute(far_out, ("ka", "fin"), other_side)
    near = lax.ppermute(near_out, "ka", pair)
    final_other = lax.ppermute(final_vectors, "vib", swap)

    partial = pl.pallas_call(
        functools.partial(own_kernel, block),
        out_shape=jax.ShapeDtypeStruct((rows, kblocks * width), F32),
        in_specs=[vmem] * 5,
        out_specs=vmem,
        scratch_shapes=[pltpu.VMEM((whole, kblocks * width), BF16)],
        cost_estimate=cost(4 * rows * whole * kblocks * width, 8 * rows * width),
        compiler_params=kernel_params(20),
        name="own",
    )(limits, moments, final_other, near_out, far_out)

    def images(is_near, is_mine, piece, base):
        shape = jax.ShapeDtypeStruct((rows, width), F32)
        if not is_mine:
            shape = jax.ShapeDtypeStruct((rows, 2 * width), BF16)
        return pl.pallas_call(
            functools.partial(image_kernel, block, is_near, is_mine),
            out_shape=shape,
            in_specs=[vmem] * 4,
            out_specs=vmem,
            cost_estimate=cost(2 * rows * rows * width, 16 * rows * width),
            compiler_params=kernel_params(20),
            name="images",
        )(limits, moments, piece, base)

    def product(is_near, halves, pairs_of, *before):
        wide = share % 128 == 0
        kernel = functools.partial(product_kernel, places, block, is_near, halves)
        if not wide:
            kernel = functools.partial(narrow_product_kernel, places, block, is_near)
        return pl.pallas_call(
            kernel,
            out_shape=[jax.ShapeDtypeStruct((half, width), F32)] * len(halves),
            in_specs=[vmem] * (2 + len(before)),
            out_specs=[vmem] * len(halves),
            scratch_shapes=[] if wide else [pltpu.VMEM((states, width), F32)],
            cost_estimate=cost(4 * rows * half * len(halves) * width, 8 * rows * width),
            compiler_params=kernel_params(20),
            name="product",
        )(initial_vectors, pairs_of, *before)

    far_other = lax.ppermute(far, "vib", swap)
    far_base = images(False, True, far, partial)
    far_images = images(False, False, far_other, far_base)
    near_other = lax.ppermute(near, "vib", swap)
    before = product(False, ("other", "own"), far_images)
    near_base = images(True, True, near, partial)
    near_images = images(True, False, near_other, near_base)
    if share % 128 == 0:
        (to_other,) = product(True, ("other",), near_images, before[0])
    else:
        to_other, to_own = product(True, ("other", "own"), near_images, *before)
    received = lax.ppermute(to_other, "vib", swap)
    if share % 128 == 0:
        (to_own,) = product(True, ("own",), near_images, before[1])
    amplitude, *coded = pl.pallas_call(
        code_kernel,
        out_shape=[jax.ShapeDtypeStruct((share, width), F32)]
        + [jax.ShapeDtypeStruct((share + SCALE_ROWS, width), jnp.int16)] * (places - 1),
        in_specs=[vmem] * 2,
        out_specs=[vmem] * places,
        cost_estimate=cost(16 * half * width, 12 * half * width),
        compiler_params=kernel_params(8),
        name="code",
    )(to_own, received)
    for s in range(1, places):
        turn = [(a, (a + s) % places) for a in range(places)]
        arrived = lax.ppermute(coded[s - 1], "ka", turn)
        amplitude = amplitude + decode(arrived, share)
    return amplitude * amplitude


def solution(mesh):
    in_specs = (
        P(None, "vib", None),
        P("ka", "vib", "grp"),
        P("ka", "vib", ("grp", "fin")),
        P(("grp", "ka")),
    )
    out_specs = P(("grp", "ka", "vib"), "fin")

    return jax.shard_map(
        on_device, mesh=mesh, in_specs=in_specs, out_specs=out_specs, check_vma=False
    )
```

time: 45.2 us -> 43.3 us (0.958)
  starting transfers between devices: 13.3 us -> 10.7 us
  local copies, waits for them, and re-layouts: 0.01 us -> 1.31 us
  Pallas kernels: 13.7 us -> 12.7 us
    ppermute x1, waiting for transfers between devices: 0.01 us -> 11.1 us  [on_device(): far = lax.ppermute(far_out, ('ka', 'fin'), other_side)]
    ppermute x1, waiting for transfers between devices: 11.9 us -> 1.41 us  [on_device(): near = lax.ppermute(near_out, 'ka', pair)]
    ppermute x3, starting transfers between devices: 8.81 us -> 5.4 us  [on_device(): arrived = lax.ppermute(coded[s - 1], 'ka', turn)]
    ppermute x1, starting transfers between devices: 0.81 us -> 2.5 us  [on_device(): far = lax.ppermute(far_out, ('ka', 'fin'), other_side)]
    unnamed x4, local copies, waits for them, and re-layouts: 0.01 us -> 1.31 us
    ppermute x1, waiting for transfers between devices: 1.85 us -> 0.73 us  [on_device(): received = lax.ppermute(to_other, 'vib', swap)]
    ppermute x1, starting transfers between devices: 2.59 us -> 1.66 us  [on_device(): near = lax.ppermute(near_out, 'ka', pair)]
    ppermute x3, waiting for transfers between devices: 3.43 us -> 4.35 us  [on_device(): arrived = lax.ppermute(coded[s - 1], 'ka', turn)]
  transfers between devices with their start and end apart: 9 -> 9, of which waited for: 3 -> 6; matrix products, arithmetic and copies ran while one was open for 0% -> 0% of each run, Pallas kernels for 23% -> 25%
where the time goes in v5:
time: 43.3 us; the launch traced here: 43.2 us
  waiting for transfers between devices  17.6 us (41%)
  Pallas kernels  12.7 us (29%)
  starting transfers between devices  10.7 us (25%)
  local copies, waits for them, and re-layouts  1.31 us (3%)
  other arithmetic  0.78 us (2%)
    ppermute x1, waiting for transfers between devices, on_device(): far = lax.ppermute(far_out, ('ka', 'fin'), other_side)  11.1 us
    ppermute x3, starting transfers between devices, on_device(): arrived = lax.ppermute(coded[s - 1], 'ka', turn)  5.4 us
    pallas_call x1, Pallas kernels, on_device(): pl.pallas_call(functools.partial(own_kernel, block), out_shape=jax.ShapeD...  4.89 us
    ppermute x3, waiting for transfers between devices, on_device(): arrived = lax.ppermute(coded[s - 1], 'ka', turn)  4.35 us
    pallas_call x4, Pallas kernels, images(): pl.pallas_call(functools.partial(image_kernel, block, is_near, is_mine),...  3.17 us
    pallas_call x3, Pallas kernels, product(): pl.pallas_call(kernel, out_shape=[jax.ShapeDtypeStruct((half, width), F32...  2.95 us
    ppermute x1, starting transfers between devices, on_device(): far = lax.ppermute(far_out, ('ka', 'fin'), other_side)  2.5 us
    ppermute x1, starting transfers between devices, on_device(): near = lax.ppermute(near_out, 'ka', pair)  1.66 us
  transfers between devices with their start and end apart: 9, of which 6 were waited for; matrix products, arithmetic and copies ran while one was open for 0% of the time, Pallas kernels for 25%

profile of v5, /device:TPU:0, one launch (start us, length us, event | category | flops | bytes accessed | tf_op | source)
XLA Modules:
  0.0 43.2 jit_solution(9854337596935631051)
XLA Ops:
  0.0 0.0 copy-start
  0.0 0.5 %collective-permute-start.2 = (bf16[2,1024,256]{2,1,0:T(8,128)(2,1)}, bf16[2,1024,256]{2,1,0:T(8,128)(2,1)S(1)}, u32[]{:S(2)}, u32[]{:S(2)}) collective-permute-start(bf16[2,1024,256]{2,1,0:T(8,128)(2,1)} %final.1), channel_id=1, source_target_pairs={{0,2},{2,0},{1,3},{3,1},{4,6},{6,4},{5,7},{7,5},{8,10},{10,8},{9,1... | collective-permute-start | bytes 3145736 | tf_op jit(solution)/shard_map/ppermute | solution.py:235
  0.5 1.5 %pack.1 = (bf16[1024,256]{1,0:T(8,128)(2,1)S(1)}, bf16[1024,256]{1,0:T(8,128)(2,1)S(1)}, s32[2,8,128]{2,1,0:T(8,128)S(1)}) custom-call(s32[2]{0:T(128)} %counts.1, bf16[2,1024,256]{2,1,0:T(8,128)(2,1)} %final.1), custom_call_target="tpu_custom_call" | custom-call | flops 4294967296 | bytes 2097152 | tf_op jit(solution)/shard_map/pack/pallas_call | solution.py:217
  2.0 2.5 %collective-permute-start.3 = (bf16[1024,256]{1,0:T(8,128)(2,1)S(1)}, bf16[1024,256]{1,0:T(8,128)(2,1)S(1)}, u32[]{:S(2)}, u32[]{:S(2)}) collective-permute-start(bf16[1024,256]{1,0:T(8,128)(2,1)S(1)} %get-tuple-element.16.far), channel_id=1, source_target_pairs={{0,1},{1,0},{4,8},{5,9},{8,4},{9,5},{12,13},{13,12},{2,3},{3,2},{6... | collective-permute-start | bytes 1572872 | tf_op jit(solution)/shard_map/ppermute | solution.py:233
  4.5 1.7 %collective-permute-start = (bf16[1024,256]{1,0:T(8,128)(2,1)S(1)}, bf16[1024,256]{1,0:T(8,128)(2,1)S(1)}, u32[]{:S(2)}, u32[]{:S(2)}) collective-permute-start(bf16[1024,256]{1,0:T(8,128)(2,1)S(1)} %get-tuple-element.15.near), channel_id=1, source_target_pairs={{0,4},{4,0},{8,12},{12,8},{1,5},{5,1},{9,13},{13,9},{2,6},{6,2},{1... | collective-permute-start | bytes 1572872 | tf_op jit(solution)/shard_map/ppermute | solution.py:234
  6.2 11.1 %collective-permute-done.3.piece = bf16[1024,256]{1,0:T(8,128)(2,1)S(1)} collective-permute-done((bf16[1024,256]{1,0:T(8,128)(2,1)S(1)}, bf16[1024,256]{1,0:T(8,128)(2,1)S(1)}, u32[]{:S(2)}, u32[]{:S(2)}) %collective-permute-start.3) | collective-permute-done | bytes 524320 | tf_op jit(solution)/shard_map/ppermute | solution.py:233
  17.2 0.0 collective-permute-start.4
  17.3 1.4 %collective-permute-done.piece = bf16[1024,256]{1,0:T(8,128)(2,1)S(1)} collective-permute-done((bf16[1024,256]{1,0:T(8,128)(2,1)S(1)}, bf16[1024,256]{1,0:T(8,128)(2,1)S(1)}, u32[]{:S(2)}, u32[]{:S(2)}) %collective-permute-start) | collective-permute-done | bytes 524320 | tf_op jit(solution)/shard_map/ppermute | solution.py:234
  18.7 0.0 collective-permute-start.1
  18.7 0.0 collective-permute-done.2.other
  18.7 0.0 copy-done
  18.7 4.9 %own.1.base = f32[1024,512]{1,0:T(8,128)S(1)} custom-call(s32[2,8,128]{2,1,0:T(8,128)S(1)} %get-tuple-element.14.limits, bf16[2,1024,2048]{2,1,0:T(8,128)(2,1)S(1)} %copy-done, bf16[2,1024,256]{2,1,0:T(8,128)(2,1)S(1)} %collective-permute-done.2.other, bf16[1024,256]{1,0:T(8,128)(2,1)S(1)} %get-tuple-element.15.near, bf16[1024,256]{1,0:T(8,128)(2,1)S(1)} %get-tuple-element.16.far), custom_call_target="tpu_custom_call" | custom-call | flops 4294967296 | bytes 2097152 | tf_op jit(solution)/shard_map/own/pallas_call | solution.py:237
  23.6 0.7 %images.6.base = f32[1024,256]{1,0:T(8,128)S(1)} custom-call(s32[2,8,128]{2,1,0:T(8,128)S(1)} %get-tuple-element.14.limits, bf16[2,1024,2048]{2,1,0:T(8,128)(2,1)S(1)} %copy-done, bf16[1024,256]{1,0:T(8,128)(2,1)S(1)} %collective-permute-done.3.piece, f32[1024,512]{1,0:T(8,128)S(1)} %own.1.base), custom_call_target="tpu_custom_call" | custom-call | flops 536870912 | bytes 4194304 | tf_op jit(solution)/shard_map/images/pallas_call | solution.py:252
  24.4 0.7 %images.4.base = f32[1024,256]{1,0:T(8,128)S(1)} custom-call(s32[2,8,128]{2,1,0:T(8,128)S(1)} %get-tuple-element.14.limits, bf16[2,1024,2048]{2,1,0:T(8,128)(2,1)S(1)} %copy-done, bf16[1024,256]{1,0:T(8,128)(2,1)S(1)} %collective-permute-done.piece, f32[1024,512]{1,0:T(8,128)S(1)} %own.1.base), custom_call_target="tpu_custom_call" | custom-call | flops 536870912 | bytes 4194304 | tf_op jit(solution)/shard_map/images/pallas_call | solution.py:252
  25.1 0.0 copy-start.1
  25.1 0.0 collective-permute-done.4.piece
  25.1 0.9 %images.7 = bf16[1024,512]{1,0:T(8,128)(2,1)S(1)} custom-call(s32[2,8,128]{2,1,0:T(8,128)S(1)} %get-tuple-element.14.limits, bf16[2,1024,2048]{2,1,0:T(8,128)(2,1)S(1)} %copy-done, bf16[1024,256]{1,0:T(8,128)(2,1)S(1)} %collective-permute-done.4.piece, f32[1024,256]{1,0:T(8,128)S(1)} %images.6.base), custom_call_target="tpu_custom_call" | custom-call | flops 536870912 | bytes 4194304 | tf_op jit(solution)/shard_map/images/pallas_call | solution.py:252
  26.0 1.3 %copy-done.1 = bf16[2,1024,1024]{2,1,0:T(8,128)(2,1)S(1)} copy-done((bf16[2,1024,1024]{2,1,0:T(8,128)(2,1)S(1)}, bf16[2,1024,1024]{2,1,0:T(8,128)(2,1)}, u32[]{:S(2)}) %copy-start.1) | copy-done | bytes 4194328
  27.3 1.3 %product.3 = (f32[512,256]{1,0:T(8,128)S(1)}, f32[512,256]{1,0:T(8,128)S(1)}) custom-call(bf16[2,1024,1024]{2,1,0:T(8,128)(2,1)S(1)} %copy-done.1, bf16[1024,512]{1,0:T(8,128)(2,1)S(1)} %images.7), custom_call_target="tpu_custom_call" | custom-call | flops 1073741824 | bytes 2097152 | tf_op jit(solution)/shard_map/product/pallas_call | solution.py:267
  28.6 0.0 collective-permute-done.1.piece
  28.7 0.9 %images.5 = bf16[1024,512]{1,0:T(8,128)(2,1)S(1)} custom-call(s32[2,8,128]{2,1,0:T(8,128)S(1)} %get-tuple-element.14.limits, bf16[2,1024,2048]{2,1,0:T(8,128)(2,1)S(1)} %copy-done, bf16[1024,256]{1,0:T(8,128)(2,1)S(1)} %collective-permute-done.1.piece, f32[1024,256]{1,0:T(8,128)S(1)} %images.4.base), custom_call_target="tpu_custom_call" | custom-call | flops 536870912 | bytes 4194304 | tf_op jit(solution)/shard_map/images/pallas_call | solution.py:252
  29.5 0.8 %product.5 = f32[512,256]{1,0:T(8,128)S(1)} custom-call(bf16[2,1024,1024]{2,1,0:T(8,128)(2,1)S(1)} %copy-done.1, bf16[1024,512]{1,0:T(8,128)(2,1)S(1)} %images.5, f32[512,256]{1,0:T(8,128)S(1)} %get-tuple-element.18.rest_0_), custom_call_target="tpu_custom_call" | custom-call | flops 536870912 | bytes 2097152 | tf_op jit(solution)/shard_map/product/pallas_call | solution.py:267
  30.3 0.6 %collective-permute-start.5 = (f32[512,256]{1,0:T(8,128)S(1)}, f32[512,256]{1,0:T(8,128)S(1)}, u32[]{:S(2)}, u32[]{:S(2)}) collective-permute-start(f32[512,256]{1,0:T(8,128)S(1)} %product.5), channel_id=1, source_target_pairs={{0,2},{2,0},{1,3},{3,1},{4,6},{6,4},{5,7},{7,5},{8,10},{10,8},{9,1... | collective-permute-start | bytes 1572872 | tf_op jit(solution)/shard_map/ppermute | solution.py:289
  30.9 0.8 %product.4.mine = f32[512,256]{1,0:T(8,128)S(1)} custom-call(bf16[2,1024,1024]{2,1,0:T(8,128)(2,1)S(1)} %copy-done.1, bf16[1024,512]{1,0:T(8,128)(2,1)S(1)} %images.5, f32[512,256]{1,0:T(8,128)S(1)} %get-tuple-element.17.rest_0_), custom_call_target="tpu_custom_call" | custom-call | flops 536870912 | bytes 2097152 | tf_op jit(solution)/shard_map/product/pallas_call | solution.py:267
  31.7 0.7 %collective-permute-done.5.other = f32[512,256]{1,0:T(8,128)S(1)} collective-permute-done((f32[512,256]{1,0:T(8,128)S(1)}, f32[512,256]{1,0:T(8,128)S(1)}, u32[]{:S(2)}, u32[]{:S(2)}) %collective-permute-start.5) | collective-permute-done | bytes 524320 | tf_op jit(solution)/shard_map/ppermute | solution.py:289
  32.4 0.2 code.1
  32.6 1.7 %collective-permute-start.6 = (s16[136,256]{1,0:T(8,128)(2,1)S(1)}, s16[136,256]{1,0:T(8,128)(2,1)S(1)}, u32[]{:S(2)}, u32[]{:S(2)}) collective-permute-start(s16[136,256]{1,0:T(8,128)(2,1)S(1)} %get-tuple-element.20), channel_id=1, source_target_pairs={{0,4},{4,8},{8,12},{12,0},{1,5},{5,9},{9,13},{13,1},{2,6},{6,10},{... | collective-permute-start | bytes 208904 | tf_op jit(solution)/shard_map/ppermute | solution.py:304
  34.4 2.5 %collective-permute-start.7 = (s16[136,256]{1,0:T(8,128)(2,1)S(1)}, s16[136,256]{1,0:T(8,128)(2,1)S(1)}, u32[]{:S(2)}, u32[]{:S(2)}) collective-permute-start(s16[136,256]{1,0:T(8,128)(2,1)S(1)} %get-tuple-element.21), channel_id=1, source_target_pairs={{0,8},{4,12},{8,0},{12,4},{1,9},{5,13},{9,1},{13,5},{2,10},{6,14},... | collective-permute-start | bytes 208904 | tf_op jit(solution)/shard_map/ppermute | solution.py:304
  36.9 1.2 %collective-permute-start.8 = (s16[136,256]{1,0:T(8,128)(2,1)S(1)}, s16[136,256]{1,0:T(8,128)(2,1)S(1)}, u32[]{:S(2)}, u32[]{:S(2)}) collective-permute-start(s16[136,256]{1,0:T(8,128)(2,1)S(1)} %get-tuple-element.22), channel_id=1, source_target_pairs={{0,12},{4,0},{8,4},{12,8},{1,13},{5,1},{9,5},{13,9},{2,14},{6,2},{... | collective-permute-start | bytes 208904 | tf_op jit(solution)/shard_map/ppermute | solution.py:304
  38.0 1.4 %collective-permute-done.6 = s16[136,256]{1,0:T(8,128)(2,1)S(1)} collective-permute-done((s16[136,256]{1,0:T(8,128)(2,1)S(1)}, s16[136,256]{1,0:T(8,128)(2,1)S(1)}, u32[]{:S(2)}, u32[]{:S(2)}) %collective-permute-start.6) | collective-permute-done | bytes 69664 | tf_op jit(solution)/shard_map/ppermute | solution.py:304
  39.4 2.7 %collective-permute-done.7 = s16[136,256]{1,0:T(8,128)(2,1)S(1)} collective-permute-done((s16[136,256]{1,0:T(8,128)(2,1)S(1)}, s16[136,256]{1,0:T(8,128)(2,1)S(1)}, u32[]{:S(2)}, u32[]{:S(2)}) %collective-permute-start.7) | collective-permute-done | bytes 69664 | tf_op jit(solution)/shard_map/ppermute | solution.py:304
  42.1 0.3 collective-permute-done.8
  42.4 0.7 %add_multiply_fusion = f32[128,256]{1,0:T(8,128)} fusion(f32[128,256]{1,0:T(8,128)S(1)} %get-tuple-element.19, s16[136,256]{1,0:T(8,128)(2,1)S(1)} %collective-permute-done.8, s16[136,256]{1,0:T(8,128)(2,1)S(1)} %collective-permute-done.7, s16[136,256]{1,0:T(8,128)(2,1)S(1)} %collective-permute-done.6, f32[256]{0:T(256)S(1)} %bitcast.5, f32[256]{0:T(256)S(1)} %bitcast.4, ...), kind=kLoop, calls=%fused_computation | loop fusion | flops 327680 | bytes 461824 | tf_op jit(solution)/shard_map/mul | solution.py:306
  (3 shorter events, 0.0 us)
Async XLA Ops:
  0.0 18.7 %copy-start = (bf16[2,1024,2048]{2,1,0:T(8,128)(2,1)S(1)}, bf16[2,1024,2048]{2,1,0:T(8,128)(2,1)}, u32[]{:S(2)}) copy-start(bf16[2,1024,2048]{2,1,0:T(8,128)(2,1)} %moments.9) | copy-start | bytes 25165828
  0.0 18.7 %collective-permute-start.2 = (bf16[2,1024,256]{2,1,0:T(8,128)(2,1)}, bf16[2,1024,256]{2,1,0:T(8,128)(2,1)S(1)}, u32[]{:S(2)}, u32[]{:S(2)}) collective-permute-start(bf16[2,1024,256]{2,1,0:T(8,128)(2,1)} %final.1), channel_id=1, source_target_pairs={{0,2},{2,0},{1,3},{3,1},{4,6},{6,4},{5,7},{7,5},{8,10},{10,8},{9,1... | collective-permute-start | bytes 3145736 | tf_op jit(solution)/shard_map/ppermute | solution.py:235
  2.0 15.2 %collective-permute-start.3 = (bf16[1024,256]{1,0:T(8,128)(2,1)S(1)}, bf16[1024,256]{1,0:T(8,128)(2,1)S(1)}, u32[]{:S(2)}, u32[]{:S(2)}) collective-permute-start(bf16[1024,256]{1,0:T(8,128)(2,1)S(1)} %get-tuple-element.16.far), channel_id=1, source_target_pairs={{0,1},{1,0},{4,8},{5,9},{8,4},{9,5},{12,13},{13,12},{2,3},{3,2},{6... | collective-permute-start | bytes 1572872 | tf_op jit(solution)/shard_map/ppermute | solution.py:233
  4.5 14.2 %collective-permute-start = (bf16[1024,256]{1,0:T(8,128)(2,1)S(1)}, bf16[1024,256]{1,0:T(8,128)(2,1)S(1)}, u32[]{:S(2)}, u32[]{:S(2)}) collective-permute-start(bf16[1024,256]{1,0:T(8,128)(2,1)S(1)} %get-tuple-element.15.near), channel_id=1, source_target_pairs={{0,4},{4,0},{8,12},{12,8},{1,5},{5,1},{9,13},{13,9},{2,6},{6,2},{1... | collective-permute-start | bytes 1572872 | tf_op jit(solution)/shard_map/ppermute | solution.py:234
  17.2 7.9 %collective-permute-start.4 = (bf16[1024,256]{1,0:T(8,128)(2,1)S(1)}, bf16[1024,256]{1,0:T(8,128)(2,1)S(1)}, u32[]{:S(2)}, u32[]{:S(2)}) collective-permute-start(bf16[1024,256]{1,0:T(8,128)(2,1)S(1)} %collective-permute-done.3.piece), channel_id=1, source_target_pairs={{0,2},{2,0},{1,3},{3,1},{4,6},{6,4},{5,7},{7,5},{8,10},{10,8},{9,1... | collective-permute-start | bytes 1572872 | tf_op jit(solution)/shard_map/ppermute | solution.py:278
  18.7 9.9 %collective-permute-start.1 = (bf16[1024,256]{1,0:T(8,128)(2,1)S(1)}, bf16[1024,256]{1,0:T(8,128)(2,1)S(1)}, u32[]{:S(2)}, u32[]{:S(2)}) collective-permute-start(bf16[1024,256]{1,0:T(8,128)(2,1)S(1)} %collective-permute-done.piece), channel_id=1, source_target_pairs={{0,2},{2,0},{1,3},{3,1},{4,6},{6,4},{5,7},{7,5},{8,10},{10,8},{9,1... | collective-permute-start | bytes 1572872 | tf_op jit(solution)/shard_map/ppermute | solution.py:281
  25.1 2.2 %copy-start.1 = (bf16[2,1024,1024]{2,1,0:T(8,128)(2,1)S(1)}, bf16[2,1024,1024]{2,1,0:T(8,128)(2,1)}, u32[]{:S(2)}) copy-start(bf16[2,1024,1024]{2,1,0:T(8,128)(2,1)} %initial.5) | copy-start | bytes 12582916
  30.3 2.1 %collective-permute-start.5 = (f32[512,256]{1,0:T(8,128)S(1)}, f32[512,256]{1,0:T(8,128)S(1)}, u32[]{:S(2)}, u32[]{:S(2)}) collective-permute-start(f32[512,256]{1,0:T(8,128)S(1)} %product.5), channel_id=1, source_target_pairs={{0,2},{2,0},{1,3},{3,1},{4,6},{6,4},{5,7},{7,5},{8,10},{10,8},{9,1... | collective-permute-start | bytes 1572872 | tf_op jit(solution)/shard_map/ppermute | solution.py:289
  32.6 6.8 %collective-permute-start.6 = (s16[136,256]{1,0:T(8,128)(2,1)S(1)}, s16[136,256]{1,0:T(8,128)(2,1)S(1)}, u32[]{:S(2)}, u32[]{:S(2)}) collective-permute-start(s16[136,256]{1,0:T(8,128)(2,1)S(1)} %get-tuple-element.20), channel_id=1, source_target_pairs={{0,4},{4,8},{8,12},{12,0},{1,5},{5,9},{9,13},{13,1},{2,6},{6,10},{... | collective-permute-start | bytes 208904 | tf_op jit(solution)/shard_map/ppermute | solution.py:304
  34.4 7.7 %collective-permute-start.7 = (s16[136,256]{1,0:T(8,128)(2,1)S(1)}, s16[136,256]{1,0:T(8,128)(2,1)S(1)}, u32[]{:S(2)}, u32[]{:S(2)}) collective-permute-start(s16[136,256]{1,0:T(8,128)(2,1)S(1)} %get-tuple-element.21), channel_id=1, source_target_pairs={{0,8},{4,12},{8,0},{12,4},{1,9},{5,13},{9,1},{13,5},{2,10},{6,14},... | collective-permute-start | bytes 208904 | tf_op jit(solution)/shard_map/ppermute | solution.py:304
  36.9 5.5 %collective-permute-start.8 = (s16[136,256]{1,0:T(8,128)(2,1)S(1)}, s16[136,256]{1,0:T(8,128)(2,1)S(1)}, u32[]{:S(2)}, u32[]{:S(2)}) collective-permute-start(s16[136,256]{1,0:T(8,128)(2,1)S(1)} %get-tuple-element.22), channel_id=1, source_target_pairs={{0,12},{4,0},{8,4},{12,8},{1,13},{5,1},{9,5},{13,9},{2,14},{6,2},{... | collective-permute-start | bytes 208904 | tf_op jit(solution)/shard_map/ppermute | solution.py:304
